TPU v7x, 32 devices: a whole 2x2x4 slice. The times are simulated.
32 devices in a mesh: row: 8 (over z, y), col: 4 (over x, core).
Axes of the slice: x: 2, y: 2, z: 4, core: 2. Of those that a mesh axis runs over, the one named last changes fastest.
Arguments:
- gradient: bfloat16 [512, 28672], P('col', 'row'), may hold values from -6 to 6
- basis: bfloat16 [28672, 28672], P('row', 'col'), may hold values from -0.03125 to 0.03125
- eigen: float32 [512, 28672], P('row', 'col'), may hold values from 0.2 to 5
Outputs:
- result: bfloat16 [512, 28672], P('col', 'row')
All inputs are finite; a program needn't handle non-finite values.
Results may differ from a plain program's by a relative error of at most 0.0044.
Values may be sent and summed in bfloat16 or wider, within the bound.
No kernel may reach another device: no remote copies, remote signals or barrier semaphores. Data moves between devices by JAX's collectives and lax.ppermute only.
A program may use at most 128 MiB of HBM per device.

v0:
```python
import functools

import jax
import jax.numpy as jnp
from jax import lax
from jax.experimental import pallas as pl
from jax.experimental.pallas import tpu as pltpu
from jax.sharding import PartitionSpec as P


F32, BF16 = jnp.float32, jnp.bfloat16
LANES = 128
ALONG = (((1,), (1,)), ((), ()))


def swap(x, axis, size, bit):
    return lax.ppermute(x, axis, [(d, d ^ (1 << bit)) for d in range(size)])


def tile_of(width, most):
    tiles = width // LANES
    return LANES * max(n for n in range(1, most // LANES + 1) if tiles % n == 0)


def pick(x, index, axis):
    return lax.dynamic_index_in_dim(x, index, axis, keepdims=False)


def in_order(mine, other, bit, axis):
    mine, other = jnp.expand_dims(mine, axis), jnp.expand_dims(other, axis)
    low = jnp.concatenate([mine, other], axis)
    high = jnp.concatenate([other, mine], axis)
    return jnp.where(bit == 0, low, high)


def general(n_row, n_col, gradient, basis, eigen):
    row_bits, col_bits = n_row.bit_length() - 1, n_col.bit_length() - 1
    r, c = lax.axis_index("row"), lax.axis_index("col")
    rbit = [(r >> b) & 1 for b in range(row_bits)]
    cbit = [(c >> b) & 1 for b in range(col_bits)]
    block = eigen.shape[0]
    w = tile_of(basis.shape[1], basis.shape[1] // 4)
    count = basis.shape[1] // w

    whole, have = gradient, []
    for b in reversed(range(col_bits)):
        got = swap(whole, "col", n_col, b)
        have = sorted(have + [b], reverse=True)
        whole = in_order(whole, got, cbit[b], have.index(b))
    whole = whole.reshape((2,) * row_bits + (block, -1))
    order = list(range(row_bits))
    k = whole.shape[-1]
    sends = pick(whole, 1 - rbit[0], row_bits - 1).reshape(-1, k)
    keeps = pick(whole, rbit[0], row_bits - 1).reshape(-1, k)

    scaled = []
    for i in range(count):
        cols = basis[:, i * w : (i + 1) * w]
        left = list(reversed(order[1:]))
        shape = (2,) * len(left) + (block, w)
        away = jnp.dot(sends, cols, preferred_element_type=F32).astype(BF16)
        mine = jnp.dot(keeps, cols, preferred_element_type=F32).reshape(shape)
        for b in order[1:]:
            total = mine + swap(away, "row", n_row, b - 1).reshape(mine.shape).astype(F32)
            axis = left.index(b)
            away, mine = pick(total, 1 - rbit[b], axis).astype(BF16), pick(total, rbit[b], axis)
            left.remove(b)
        total = mine + swap(away, "row", n_row, order[-1]).reshape(mine.shape).astype(F32)
        part, have = (total / eigen[:, i * w : (i + 1) * w]).astype(BF16), []
        for b in reversed(order):
            got = swap(part, "row", n_row, b)
            have = sorted(have + [b], reverse=True)
            part = in_order(part, got, rbit[b], have.index(b))
        scaled.append(part.reshape(n_row * block, w))

    out = None
    for i in range(count):
        cols = basis[:, i * w : (i + 1) * w]
        term = lax.dot_general(scaled[i], cols, ALONG, preferred_element_type=F32)
        out = term if out is None else out + term
    out = out.reshape((2,) * col_bits + (gradient.shape[0], -1))
    left = list(reversed(range(col_bits)))
    for b in range(col_bits):
        axis = left.index(b)
        away, mine = pick(out, 1 - cbit[b], axis).astype(BF16), pick(out, cbit[b], axis)
        out = mine + swap(away, "col", n_col, b).astype(F32)
        left.remove(b)
    return out.astype(BF16)


def copy_block(sources, which, at, rows, to, slot):
    at = pl.multiple_of(at * rows, rows)
    for d, source in enumerate(sources):

        @pl.when(which == d)
        def _():
            to[pl.ds(slot * rows, rows), :] = source[pl.ds(at, rows), :]


def rotate_body(bits, block, n, idx, *refs):
    shards, (b, away, keep, rows) = refs[:n], refs[n:]
    slots = 1 << len(bits)

    @pl.when(pl.program_id(0) == 0)
    def _():
        for slot in range(slots):
            p = {bit: slot >> (len(bits) - 1 - j) & 1 for j, bit in enumerate(bits)}
            which = idx[1] ^ p[1]
            if 2 in p:
                which = which + 2 * (idx[2] ^ p[2])
            copy_block(shards, which, idx[0] ^ p[0], block, rows, slot)

    out = jnp.dot(rows[...], b[...], preferred_element_type=F32)
    half = slots // 2 * block
    keep[...] = out[:half]
    away[...] = out[half:].astype(BF16)


def fixed(shape):
    return pl.BlockSpec(shape, lambda i, idx: (0, 0), pipeline_mode=pl.Buffered(1))


def rotate(idx, shards, basis, start, w, bits, block):
    k = shards[0].shape[1]
    tile = tile_of(w, 896)
    first = start // tile
    count = block << len(bits)
    rows = pl.BlockSpec((count // 2, tile), lambda i, idx: (0, i))
    return pl.pallas_call(
        functools.partial(rotate_body, bits, block, len(shards)),
        grid_spec=pltpu.PrefetchScalarGridSpec(
            num_scalar_prefetch=1,
            grid=(w // tile,),
            in_specs=[fixed(x.shape) for x in shards]
            + [pl.BlockSpec((k, tile), lambda i, idx: (0, i + first))],
            out_specs=[rows, rows],
            scratch_shapes=[pltpu.VMEM((count, k), BF16)],
        ),
        out_shape=[
            jax.ShapeDtypeStruct((count // 2, w), BF16),
            jax.ShapeDtypeStruct((count // 2, w), F32),
        ],
        compiler_params=pltpu.CompilerParams(vmem_limit_bytes=30 << 20),
        cost_estimate=pl.CostEstimate(
            flops=2 * count * k * w, bytes_accessed=2 * k * w, transcendentals=0
        ),
        name="rotate",
    )(idx, *shards, basis)


def back_body(bits, block, more, idx, lo, hi, b, *refs):
    parts = 1 << len(bits) - 1
    rows, outs, before = refs[-1], refs[-1 - parts : -1], refs[:parts]

    @pl.when(pl.program_id(0) == 0)
    def _():
        for slot in range(2 * parts):
            p = {bit: idx[bit] ^ (slot >> bit & 1) for bit in bits}
            at = p[bits[1]] if len(bits) == 2 else 2 * p[bits[1]] + p[bits[2]]
            copy_block((lo, hi), p[bits[0]], at, block, rows, slot)

    out = lax.dot_general(rows[...], b[...], ALONG, preferred_element_type=F32)
    for n in range(parts):
        part = out[2 * n * block : 2 * (n + 1) * block]
        if more:
            part = part + before[n][...]
        outs[n][...] = part.astype(outs[n].dtype)


def back(idx, lo, hi, basis, start, w, bits, block, before, last):
    k = basis.shape[0]
    tile = tile_of(k, 896)
    rows = pl.BlockSpec((2 * block, tile), lambda i, idx: (0, i))
    parts = 1 << len(bits) - 1
    return pl.pallas_call(
        functools.partial(back_body, bits, block, len(before) > 0),
        grid_spec=pltpu.PrefetchScalarGridSpec(
            num_scalar_prefetch=1,
            grid=(k // tile,),
            in_specs=[
                fixed(lo.shape),
                fixed(hi.shape),
                pl.BlockSpec((tile, w), lambda i, idx: (i, start // w)),
            ]
            + [rows] * len(before),
            out_specs=[rows] * parts,
            scratch_shapes=[pltpu.VMEM((2 * lo.shape[0], w), BF16)],
        ),
        out_shape=[
            jax.ShapeDtypeStruct((2 * block, k), BF16 if last and n % 2 else F32)
            for n in range(parts)
        ],
        compiler_params=pltpu.CompilerParams(vmem_limit_bytes=24 << 20),
        cost_estimate=pl.CostEstimate(
            flops=4 * lo.shape[0] * k * w, bytes_accessed=2 * k * w, transcendentals=0
        ),
        name="back",
    )(idx, lo, hi, basis, *before)


def columns(body, idx, ins, outs):
    w = outs[0].shape[1]
    tile = tile_of(w, 1792)
    specs = [
        pl.BlockSpec((x.shape[0], tile), functools.partial(lambda f, i, idx: (0, i + f), start // tile))
        for x, start in ins
    ]
    moved = sum(x.shape[0] * w * x.dtype.itemsize for x, _ in ins)
    return pl.pallas_call(
        body,
        grid_spec=pltpu.PrefetchScalarGridSpec(
            num_scalar_prefetch=1,
            grid=(w // tile,),
            in_specs=specs,
            out_specs=[pl.BlockSpec((o.shape[0], tile), lambda i, idx: (0, i)) for o in outs],
        ),
        out_shape=outs,
        compiler_params=pltpu.CompilerParams(vmem_limit_bytes=24 << 20),
        cost_estimate=pl.CostEstimate(flops=moved, bytes_accessed=2 * moved, transcendentals=0),
    )(idx, *[x for x, _ in ins])


def sum_body(idx, keep, got, away):
    away[...] = (keep[...] + got[...].astype(F32)).astype(BF16)


def three(keep, a, b, rows):
    return keep[rows, :] + a[rows, :].astype(F32) + b[rows, :].astype(F32)


def halve_body(idx, keep, got, more, keep2, away2):
    half = keep2.shape[0]
    keep2[...] = three(keep, got, more, slice(0, half))
    away2[...] = three(keep, got, more, slice(half, 2 * half)).astype(BF16)


def merge_body(idx, own, own_y, own_e, far, far_y, far_e, keep, away):
    a = three(own, own_y, own_e, slice(None))
    b = three(far, far_y, far_e, slice(None))
    straight = idx[2] == 0
    keep[...] = jnp.where(straight, a, b)
    away[...] = jnp.where(straight, b, a).astype(BF16)


def scale_body(idx, keep, got, mine, other, out):
    block = mine.shape[0]
    low = idx[3] == 0
    total = keep[...] + got[...].astype(F32)
    first = jnp.where(low, mine[...], other[...])
    second = jnp.where(low, other[...], mine[...])
    out[:block, :] = (total[:block] / first).astype(BF16)
    out[block:, :] = (total[block:] / second).astype(BF16)


def inner(idx, a, b):
    return jnp.where(idx[4] == 1, a[...], b[...])


def join_body(idx, near, away, near_out, away_out, out):
    half = near.shape[0]
    out[:half, :] = inner(idx, near, near_out)
    out[half:, :] = inner(idx, away, away_out)


def part_body(idx, near, away, near_out, away_out, own, far):
    a, b = inner(idx, near, near_out), inner(idx, away, away_out)
    straight = idx[2] == 0
    own[...] = jnp.where(straight, a, b)
    far[...] = jnp.where(straight, b, a)


def add_body(idx, keep, got, out):
    out[...] = (keep[...] + got[...].astype(F32)).astype(BF16)


def last_body(idx, keep, got, far, out):
    out[...] = (keep[...] + got[...].astype(F32) + far[...].astype(F32)).astype(BF16)


def paired(n_row, n_col, chunks, gradient, basis, eigen):
    r, c = lax.axis_index("row"), lax.axis_index("col")
    bits = [r & 1, c & 1, ((r >> 2) ^ (c >> 1)) & 1, (r >> 1) & 1, ((r >> 2) ^ (r >> 1)) & 1]
    idx = jnp.stack(bits).astype(jnp.int32)
    block = eigen.shape[0]
    w = eigen.shape[1] // len(chunks)
    s = jax.ShapeDtypeStruct
    mid = [d for d in range(n_row) if (d >> 2 ^ d >> 1) & 1]
    inwards = [(d ^ 2, d) for d in mid]
    outwards = [(d, d ^ 2) for d in mid]
    across = [(d, d ^ 6) for d in mid]

    def send(x, pairs):
        return lax.ppermute(x, "row", pairs)

    def row(x):
        return swap(x, "row", n_row, 0)

    def col(x, bit):
        return swap(x, "col", n_col, bit)

    def cols(body, ins, outs):
        ins = [x if isinstance(x, tuple) else (x, 0) for x in ins]
        outs = [s((rows, w), kind) for rows, kind in outs]
        out = columns(body, idx, ins, outs)
        return out if len(outs) > 1 else out[0]

    far_half = col(gradient, 1)
    shards = {"own": (gradient, col(gradient, 0)), "far": (far_half, col(far_half, 0))}
    other = send(eigen, inwards)

    def rotated(held, start, order):
        away, keep = rotate(idx, held, basis, start, w, order, block)
        got = row(away)
        total = cols(sum_body, [keep, got], [(keep.shape[0], BF16)])
        return [keep, got, send(total, inwards)]

    held = {}
    halves = [(2 * block, F32), (2 * block, BF16)]
    for i, (cut, _) in enumerate(chunks):
        if cut:
            part = rotated(shards["own"], i * w, (0, 1))
            part += rotated(shards["far"], i * w, (0, 1))
            keep, away = cols(merge_body, part, halves)
        else:
            part = rotated(shards["own"] + shards["far"], i * w, (0, 2, 1))
            keep, away = cols(halve_body, part, halves)
        got = send(away, across)
        held[i] = cols(scale_body, [keep, got, (eigen, i * w), (other, i * w)], halves[1:])

    done = ()
    for i, (_, cut) in enumerate(chunks):
        near = held[i]
        away = send(near, across)
        near_out = send(near, outwards)
        parts = [near, away, near_out, send(away, outwards)]
        last = i == len(chunks) - 1
        if not cut:
            lo = cols(join_body, parts, [(4 * block, BF16)])
            hi = row(lo)
            done = back(idx, lo, hi, basis, i * w, w, (0, 2, 1), block, done, last)
            continue
        own, far = cols(part_body, parts, [(2 * block, BF16)] * 2)
        parts = []
        for lo, before in ((own, done[:2]), (far, done[2:])):
            hi = row(lo)
            parts += back(idx, lo, hi, basis, i * w, w, (0, 1), block, before, last)
        done = tuple(parts)

    def final(body, ins):
        outs = [s(gradient.shape, BF16)]
        return columns(body, idx, [(x, 0) for x in ins], outs)[0]

    far = final(add_body, [done[2], col(done[3], 0)])
    far = col(far, 1)
    return final(last_body, [done[0], col(done[1], 0), far])


CHUNKS = (
    (True, False),
    (True, False),
    (False, True),
    (False, True),
)


def solution(mesh):
    n_row, n_col = mesh.shape["row"], mesh.shape["col"]
    fits = n_row == 2 * n_col and n_col.bit_length() == 3

    def per_device(gradient, basis, eigen):
        if fits:
            return paired(n_row, n_col, CHUNKS, gradient, basis, eigen)
        return general(n_row, n_col, gradient, basis, eigen)

    return jax.shard_map(
        per_device,
        mesh=mesh,
        in_specs=(P("col", "row"), P("row", "col"), P("row", "col")),
        out_specs=P("col", "row"),
        check_vma=False,
    )
```

profile of v0, /device:TPU:0, one launch (start us, length us, event | category | flops | bytes accessed | tf_op | source)
XLA Modules:
  0.0 331.5 jit_solution(17535246692044014759)
XLA Ops:
  0.0 3.0 collective-permute-start.1
  3.0 20.6 %collective-permute-done.1.refs_2_.refs_0_ = bf16[128,3584]{1,0:T(8,128)(2,1)S(1)} collective-permute-done((bf16[128,3584]{1,0:T(8,128)(2,1)}, bf16[128,3584]{1,0:T(8,128)(2,1)S(1)}, u32[]{:S(2)}, u32[]{:S(2)}) %collective-permute-start.1) | collective-permute-done | bytes 917536 | tf_op jit(solution)/shard_map/ppermute | solution.py:17
  24.9 8.0 %rotate.10 = (bf16[128,1792]{1,0:T(8,128)(2,1)S(1)}, f32[128,1792]{1,0:T(8,128)S(1)}) custom-call(s32[5]{0:T(128)S(1)} %stack.23.idx, bf16[128,3584]{1,0:T(8,128)(2,1)S(1)} %copy-done.1, bf16[128,3584]{1,0:T(8,128)(2,1)S(1)} %collective-permute-done.refs_1_, bf16[3584,7168]{1,0:T(8,128)(2,1)} %b.11), custom_call_target="tpu_custom_call" | custom-call | flops 3288334336 | bytes 12845056 | tf_op jit(solution)/shard_map/rotate/pallas_call | solution.py:129
  32.9 1.8 collective-permute-start.27
  34.8 3.6 %collective-permute-start.6 = (f32[64,7168]{1,0:T(8,128)S(1)}, f32[64,7168]{1,0:T(8,128)S(1)}, u32[]{:S(2)}, u32[]{:S(2)}) collective-permute-start(f32[64,7168]{1,0:T(8,128)S(1)} %copy-done), channel_id=1, source_target_pairs={{0,8},{4,12},{24,16},{28,20},{1,9},{5,13},{25,17},{29,21},{2,10},{... | collective-permute-start | bytes 5505032 | tf_op jit(solution)/shard_map/ppermute | solution.py:293
  38.3 7.8 %rotate.8 = (bf16[128,1792]{1,0:T(8,128)(2,1)S(1)}, f32[128,1792]{1,0:T(8,128)S(1)}) custom-call(s32[5]{0:T(128)S(1)} %stack.23.idx, bf16[128,3584]{1,0:T(8,128)(2,1)S(1)} %copy-done.1, bf16[128,3584]{1,0:T(8,128)(2,1)S(1)} %collective-permute-done.refs_1_, bf16[3584,7168]{1,0:T(8,128)(2,1)} %b.11), custom_call_target="tpu_custom_call" | custom-call | flops 3288334336 | bytes 12845056 | tf_op jit(solution)/shard_map/rotate/pallas_call | solution.py:129
  47.4 3.1 collective-permute-start.28
  50.5 8.0 %rotate.11 = (bf16[128,1792]{1,0:T(8,128)(2,1)S(1)}, f32[128,1792]{1,0:T(8,128)S(1)}) custom-call(s32[5]{0:T(128)S(1)} %stack.23.idx, bf16[128,3584]{1,0:T(8,128)(2,1)S(1)} %collective-permute-done.1.refs_2_.refs_0_, bf16[128,3584]{1,0:T(8,128)(2,1)S(1)} %collective-permute-done.2.refs_3_.refs_1_, bf16[3584,7168]{1,0:T(8,128)(2,1)} %b.11), custom_call_target="tpu_custom_call" | custom-call | flops 3288334336 | bytes 12845056 | tf_op jit(solution)/shard_map/rotate/pallas_call | solution.py:129
  58.4 2.0 collective-permute-start.29
  60.5 12.0 %rotate.6 = (bf16[256,1792]{1,0:T(8,128)(2,1)S(1)}, f32[256,1792]{1,0:T(8,128)S(1)}) custom-call(s32[5]{0:T(128)S(1)} %stack.23.idx, bf16[128,3584]{1,0:T(8,128)(2,1)S(1)} %copy-done.2, bf16[128,3584]{1,0:T(8,128)(2,1)S(1)} %collective-permute-done.refs_1_, bf16[128,3584]{1,0:T(8,128)(2,1)S(1)} %collective-permute-done.1.refs_2_.refs_0_, ...), custom_call_target="tpu_custom_call" | custom-call | flops 6576668672 | bytes 12845056 | tf_op jit(solution)/shard_map/rotate/pallas_call | solution.py:129
  74.7 12.0 %rotate.7 = (bf16[256,1792]{1,0:T(8,128)(2,1)S(1)}, f32[256,1792]{1,0:T(8,128)S(1)}) custom-call(s32[5]{0:T(128)S(1)} %stack.23.idx, bf16[128,3584]{1,0:T(8,128)(2,1)S(1)} %copy-done.2, bf16[128,3584]{1,0:T(8,128)(2,1)S(1)} %collective-permute-done.refs_1_, bf16[128,3584]{1,0:T(8,128)(2,1)S(1)} %collective-permute-done.1.refs_2_.refs_0_, ...), custom_call_target="tpu_custom_call" | custom-call | flops 6576668672 | bytes 12845056 | tf_op jit(solution)/shard_map/rotate/pallas_call | solution.py:129
  86.7 1.7 collective-permute-done.28.own_e
  89.0 7.8 %rotate.9 = (bf16[128,1792]{1,0:T(8,128)(2,1)S(1)}, f32[128,1792]{1,0:T(8,128)S(1)}) custom-call(s32[5]{0:T(128)S(1)} %stack.23.idx, bf16[128,3584]{1,0:T(8,128)(2,1)S(1)} %collective-permute-done.1.refs_2_.refs_0_, bf16[128,3584]{1,0:T(8,128)(2,1)S(1)} %collective-permute-done.2.refs_3_.refs_1_, bf16[3584,7168]{1,0:T(8,128)(2,1)} %b.11), custom_call_target="tpu_custom_call" | custom-call | flops 3288334336 | bytes 12845056 | tf_op jit(solution)/shard_map/rotate/pallas_call | solution.py:129
  100.6 22.3 %collective-permute-done.20.got.far_y = bf16[128,1792]{1,0:T(8,128)(2,1)S(1)} collective-permute-done((bf16[128,1792]{1,0:T(8,128)(2,1)S(1)}, bf16[128,1792]{1,0:T(8,128)(2,1)S(1)}, u32[]{:S(2)}, u32[]{:S(2)}) %collective-permute-start.20) | collective-permute-done | bytes 458784 | tf_op jit(solution)/shard_map/ppermute | solution.py:17
  132.0 3.3 %collective-permute-done.19.own_e = bf16[128,1792]{1,0:T(8,128)(2,1)S(1)} collective-permute-done((bf16[128,1792]{1,0:T(8,128)(2,1)S(1)}, bf16[128,1792]{1,0:T(8,128)(2,1)S(1)}, u32[]{:S(2)}, u32[]{:S(2)}) %collective-permute-start.19) | collective-permute-done | bytes 458784 | tf_op jit(solution)/shard_map/ppermute | solution.py:293
  135.3 9.8 %collective-permute-done.21.far_e = bf16[128,1792]{1,0:T(8,128)(2,1)S(1)} collective-permute-done((bf16[128,1792]{1,0:T(8,128)(2,1)S(1)}, bf16[128,1792]{1,0:T(8,128)(2,1)S(1)}, u32[]{:S(2)}, u32[]{:S(2)}) %collective-permute-start.21) | collective-permute-done | bytes 458784 | tf_op jit(solution)/shard_map/ppermute | solution.py:293
  150.8 14.0 %collective-permute-done.4.more = bf16[256,1792]{1,0:T(8,128)(2,1)S(1)} collective-permute-done((bf16[256,1792]{1,0:T(8,128)(2,1)S(1)}, bf16[256,1792]{1,0:T(8,128)(2,1)S(1)}, u32[]{:S(2)}, u32[]{:S(2)}) %collective-permute-start.4) | collective-permute-done | bytes 917536 | tf_op jit(solution)/shard_map/ppermute | solution.py:293
  166.3 15.9 %collective-permute-done.12.more = bf16[256,1792]{1,0:T(8,128)(2,1)S(1)} collective-permute-done((bf16[256,1792]{1,0:T(8,128)(2,1)S(1)}, bf16[256,1792]{1,0:T(8,128)(2,1)S(1)}, u32[]{:S(2)}, u32[]{:S(2)}) %collective-permute-start.12) | collective-permute-done | bytes 917536 | tf_op jit(solution)/shard_map/ppermute | solution.py:293
  190.4 12.4 %collective-permute-done.24.near_out = bf16[128,1792]{1,0:T(8,128)(2,1)S(1)} collective-permute-done((bf16[128,1792]{1,0:T(8,128)(2,1)S(1)}, bf16[128,1792]{1,0:T(8,128)(2,1)S(1)}, u32[]{:S(2)}, u32[]{:S(2)}) %collective-permute-start.24) | collective-permute-done | bytes 458784 | tf_op jit(solution)/shard_map/ppermute | solution.py:293
  202.8 6.4 %collective-permute-done.25.away_out = bf16[128,1792]{1,0:T(8,128)(2,1)S(1)} collective-permute-done((bf16[128,1792]{1,0:T(8,128)(2,1)S(1)}, bf16[128,1792]{1,0:T(8,128)(2,1)S(1)}, u32[]{:S(2)}, u32[]{:S(2)}) %collective-permute-start.25) | collective-permute-done | bytes 458784 | tf_op jit(solution)/shard_map/ppermute | solution.py:293
  216.8 11.5 %back.6 = (f32[128,3584]{1,0:T(8,128)S(1)}, f32[128,3584]{1,0:T(8,128)S(1)}, f32[128,3584]{1,0:T(8,128)S(1)}, f32[128,3584]{1,0:T(8,128)S(1)}) custom-call(s32[5]{0:T(128)S(1)} %stack.23.idx, bf16[256,1792]{1,0:T(8,128)(2,1)S(1)} %shard_map.54.lo, bf16[256,1792]{1,0:T(8,128)(2,1)S(1)} %collective-permute-done.35.hi, bf16[3584,7168]{1,0:T(8,128)(2,1)} %b.11), custom_call_target="tpu_custom_call" | custom-call | flops 6576668672 | bytes 12845056 | tf_op jit(solution)/shard_map/back/pallas_call | solution.py:175
  228.4 17.9 %collective-permute-done.9.away_out = bf16[128,1792]{1,0:T(8,128)(2,1)S(1)} collective-permute-done((bf16[128,1792]{1,0:T(8,128)(2,1)S(1)}, bf16[128,1792]{1,0:T(8,128)(2,1)S(1)}, u32[]{:S(2)}, u32[]{:S(2)}) %collective-permute-start.9) | collective-permute-done | bytes 458784 | tf_op jit(solution)/shard_map/ppermute | solution.py:293
  247.6 4.0 %collective-permute-done.16.away_out = bf16[128,1792]{1,0:T(8,128)(2,1)S(1)} collective-permute-done((bf16[128,1792]{1,0:T(8,128)(2,1)S(1)}, bf16[128,1792]{1,0:T(8,128)(2,1)S(1)}, u32[]{:S(2)}, u32[]{:S(2)}) %collective-permute-start.16) | collective-permute-done | bytes 458784 | tf_op jit(solution)/shard_map/ppermute | solution.py:293
  252.8 11.9 %back.7 = (f32[128,3584]{1,0:T(8,128)S(1)}, f32[128,3584]{1,0:T(8,128)S(1)}, f32[128,3584]{1,0:T(8,128)S(1)}, f32[128,3584]{1,0:T(8,128)S(1)}) custom-call(s32[5]{0:T(128)S(1)} %stack.23.idx, bf16[256,1792]{1,0:T(8,128)(2,1)S(1)} %shard_map.49.lo, bf16[256,1792]{1,0:T(8,128)(2,1)S(1)} %collective-permute-done.26.hi, bf16[3584,7168]{1,0:T(8,128)(2,1)} %b.11, ...), custom_call_target="tpu_custom_call" | custom-call | flops 6576668672 | bytes 12845056 | tf_op jit(solution)/shard_map/back/pallas_call | solution.py:175
  267.7 8.3 %back.10 = (f32[128,3584]{1,0:T(8,128)S(1)}, f32[128,3584]{1,0:T(8,128)S(1)}) custom-call(s32[5]{0:T(128)S(1)} %stack.23.idx, bf16[128,1792]{1,0:T(8,128)(2,1)S(1)} %get-tuple-element.78.lo, bf16[128,1792]{1,0:T(8,128)(2,1)S(1)} %collective-permute-done.38.hi, bf16[3584,7168]{1,0:T(8,128)(2,1)} %b.11, f32[128,3584]{1,0:T(8,128)S(1)} %get-tuple-element.79.refs_0_, ...), custom_call_target="tpu_custom_call" | custom-call | flops 3288334336 | bytes 12845056 | tf_op jit(solution)/shard_map/back/pallas_call | solution.py:175
  276.0 8.3 %back.11 = (f32[128,3584]{1,0:T(8,128)S(1)}, bf16[128,3584]{1,0:T(8,128)(2,1)S(1)}) custom-call(s32[5]{0:T(128)S(1)} %stack.23.idx, bf16[128,1792]{1,0:T(8,128)(2,1)S(1)} %get-tuple-element.77.lo, bf16[128,1792]{1,0:T(8,128)(2,1)S(1)} %collective-permute-done.37.hi, bf16[3584,7168]{1,0:T(8,128)(2,1)} %b.11, f32[128,3584]{1,0:T(8,128)S(1)} %get-tuple-element.81.refs_0_, ...), custom_call_target="tpu_custom_call" | custom-call | flops 3288334336 | bytes 12845056 | tf_op jit(solution)/shard_map/back/pallas_call | solution.py:175
  284.5 8.3 %back.8 = (f32[128,3584]{1,0:T(8,128)S(1)}, f32[128,3584]{1,0:T(8,128)S(1)}) custom-call(s32[5]{0:T(128)S(1)} %stack.23.idx, bf16[128,1792]{1,0:T(8,128)(2,1)S(1)} %get-tuple-element.54.lo, bf16[128,1792]{1,0:T(8,128)(2,1)S(1)} %collective-permute-done.17.hi, bf16[3584,7168]{1,0:T(8,128)(2,1)} %b.11, f32[128,3584]{1,0:T(8,128)S(1)} %get-tuple-element.71.refs_0_, ...), custom_call_target="tpu_custom_call" | custom-call | flops 3288334336 | bytes 12845056 | tf_op jit(solution)/shard_map/back/pallas_call | solution.py:175
  292.9 4.5 %collective-permute-done.10.hi = bf16[128,1792]{1,0:T(8,128)(2,1)S(1)} collective-permute-done((bf16[128,1792]{1,0:T(8,128)(2,1)S(1)}, bf16[128,1792]{1,0:T(8,128)(2,1)S(1)}, u32[]{:S(2)}, u32[]{:S(2)}) %collective-permute-start.10) | collective-permute-done | bytes 458784 | tf_op jit(solution)/shard_map/ppermute | solution.py:17
  297.4 8.3 %back.9 = (f32[128,3584]{1,0:T(8,128)S(1)}, bf16[128,3584]{1,0:T(8,128)(2,1)S(1)}) custom-call(s32[5]{0:T(128)S(1)} %stack.23.idx, bf16[128,1792]{1,0:T(8,128)(2,1)S(1)} %get-tuple-element.49.lo, bf16[128,1792]{1,0:T(8,128)(2,1)S(1)} %collective-permute-done.10.hi, bf16[3584,7168]{1,0:T(8,128)(2,1)} %b.11, f32[128,3584]{1,0:T(8,128)S(1)} %get-tuple-element.73.refs_0_, ...), custom_call_target="tpu_custom_call" | custom-call | flops 3288334336 | bytes 12845056 | tf_op jit(solution)/shard_map/back/pallas_call | solution.py:175
  306.8 1.6 collective-permute-start.40
  308.4 21.2 %collective-permute-done.40.far = bf16[128,3584]{1,0:T(8,128)(2,1)S(1)} collective-permute-done((bf16[128,3584]{1,0:T(8,128)(2,1)S(1)}, bf16[128,3584]{1,0:T(8,128)(2,1)S(1)}, u32[]{:S(2)}, u32[]{:S(2)}) %collective-permute-start.40) | collective-permute-done | bytes 917536 | tf_op jit(solution)/shard_map/ppermute | solution.py:17
  329.6 1.9 shard_map.56
  (89 shorter events, 47.5 us)
Async XLA Ops:
  0.0 23.5 %collective-permute-start.1 = (bf16[128,3584]{1,0:T(8,128)(2,1)}, bf16[128,3584]{1,0:T(8,128)(2,1)S(1)}, u32[]{:S(2)}, u32[]{:S(2)}) collective-permute-start(bf16[128,3584]{1,0:T(8,128)(2,1)} %refs_0_.7), channel_id=1, source_target_pairs={{0,2},{1,3},{2,0},{3,1},{4,6},{5,7},{6,4},{7,5},{8,10},{9,11},{10,... | collective-permute-start | bytes 2752520 | tf_op jit(solution)/shard_map/ppermute | solution.py:17
  3.0 20.6 %collective-permute-start = (bf16[128,3584]{1,0:T(8,128)(2,1)}, bf16[128,3584]{1,0:T(8,128)(2,1)S(1)}, u32[]{:S(2)}, u32[]{:S(2)}) collective-permute-start(bf16[128,3584]{1,0:T(8,128)(2,1)} %refs_0_.7), channel_id=1, source_target_pairs={{0,1},{1,0},{2,3},{3,2},{4,5},{5,4},{6,7},{7,6},{8,9},{9,8},{10,11... | collective-permute-start | bytes 2752520 | tf_op jit(solution)/shard_map/ppermute | solution.py:17
  23.5 26.9 %collective-permute-start.2 = (bf16[128,3584]{1,0:T(8,128)(2,1)S(1)}, bf16[128,3584]{1,0:T(8,128)(2,1)S(1)}, u32[]{:S(2)}, u32[]{:S(2)}) collective-permute-start(bf16[128,3584]{1,0:T(8,128)(2,1)S(1)} %collective-permute-done.1.refs_2_.refs_0_), channel_id=1, source_target_pairs={{0,1},{1,0},{2,3},{3,2},{4,5},{5,4},{6,7},{7,6},{8,9},{9,8},{10,11... | collective-permute-start | bytes 2752520 | tf_op jit(solution)/shard_map/ppermute | solution.py:17
  34.8 94.4 %collective-permute-start.6 = (f32[64,7168]{1,0:T(8,128)S(1)}, f32[64,7168]{1,0:T(8,128)S(1)}, u32[]{:S(2)}, u32[]{:S(2)}) collective-permute-start(f32[64,7168]{1,0:T(8,128)S(1)} %copy-done), channel_id=1, source_target_pairs={{0,8},{4,12},{24,16},{28,20},{1,9},{5,13},{25,17},{29,21},{2,10},{... | collective-permute-start | bytes 5505032 | tf_op jit(solution)/shard_map/ppermute | solution.py:293
  46.2 53.1 %collective-permute-start.18 = (bf16[128,1792]{1,0:T(8,128)(2,1)S(1)}, bf16[128,1792]{1,0:T(8,128)(2,1)S(1)}, u32[]{:S(2)}, u32[]{:S(2)}) collective-permute-start(bf16[128,1792]{1,0:T(8,128)(2,1)S(1)} %get-tuple-element.56), channel_id=1, source_target_pairs={{0,4},{4,0},{8,12},{12,8},{16,20},{20,16},{24,28},{28,24},{1,5},{5... | collective-permute-start | bytes 1376264 | tf_op jit(solution)/shard_map/ppermute | solution.py:17
  47.4 41.1 %collective-permute-start.28 = (bf16[128,1792]{1,0:T(8,128)(2,1)S(1)}, bf16[128,1792]{1,0:T(8,128)(2,1)S(1)}, u32[]{:S(2)}, u32[]{:S(2)}) collective-permute-start(bf16[128,1792]{1,0:T(8,128)(2,1)S(1)} %shard_map.50), channel_id=1, source_target_pairs={{0,8},{4,12},{24,16},{28,20},{1,9},{5,13},{25,17},{29,21},{2,10},{... | collective-permute-start | bytes 1376264 | tf_op jit(solution)/shard_map/ppermute | solution.py:293
  72.5 52.6 %collective-permute-start.3 = (bf16[256,1792]{1,0:T(8,128)(2,1)S(1)}, bf16[256,1792]{1,0:T(8,128)(2,1)S(1)}, u32[]{:S(2)}, u32[]{:S(2)}) collective-permute-start(bf16[256,1792]{1,0:T(8,128)(2,1)S(1)} %get-tuple-element.46), channel_id=1, source_target_pairs={{0,4},{4,0},{8,12},{12,8},{16,20},{20,16},{24,28},{28,24},{1,5},{5... | collective-permute-start | bytes 2752520 | tf_op jit(solution)/shard_map/ppermute | solution.py:17
  73.2 24.3 %collective-permute-start.30 = (bf16[128,1792]{1,0:T(8,128)(2,1)S(1)}, bf16[128,1792]{1,0:T(8,128)(2,1)S(1)}, u32[]{:S(2)}, u32[]{:S(2)}) collective-permute-start(bf16[128,1792]{1,0:T(8,128)(2,1)S(1)} %shard_map.51), channel_id=1, source_target_pairs={{0,8},{4,12},{24,16},{28,20},{1,9},{5,13},{25,17},{29,21},{2,10},{... | collective-permute-start | bytes 1376264 | tf_op jit(solution)/shard_map/ppermute | solution.py:293
  88.4 38.7 %collective-permute-start.11 = (bf16[256,1792]{1,0:T(8,128)(2,1)S(1)}, bf16[256,1792]{1,0:T(8,128)(2,1)S(1)}, u32[]{:S(2)}, u32[]{:S(2)}) collective-permute-start(bf16[256,1792]{1,0:T(8,128)(2,1)S(1)} %get-tuple-element.51), channel_id=1, source_target_pairs={{0,4},{4,0},{8,12},{12,8},{16,20},{20,16},{24,28},{28,24},{1,5},{5... | collective-permute-start | bytes 2752520 | tf_op jit(solution)/shard_map/ppermute | solution.py:17
  97.5 25.4 %collective-permute-start.20 = (bf16[128,1792]{1,0:T(8,128)(2,1)S(1)}, bf16[128,1792]{1,0:T(8,128)(2,1)S(1)}, u32[]{:S(2)}, u32[]{:S(2)}) collective-permute-start(bf16[128,1792]{1,0:T(8,128)(2,1)S(1)} %get-tuple-element.58), channel_id=1, source_target_pairs={{0,4},{4,0},{8,12},{12,8},{16,20},{20,16},{24,28},{28,24},{1,5},{5... | collective-permute-start | bytes 1376264 | tf_op jit(solution)/shard_map/ppermute | solution.py:17
  99.2 31.3 %collective-permute-start.31 = (bf16[128,1792]{1,0:T(8,128)(2,1)S(1)}, bf16[128,1792]{1,0:T(8,128)(2,1)S(1)}, u32[]{:S(2)}, u32[]{:S(2)}) collective-permute-start(bf16[128,1792]{1,0:T(8,128)(2,1)S(1)} %get-tuple-element.66), channel_id=1, source_target_pairs={{8,16},{12,20},{16,8},{20,12},{9,17},{13,21},{17,9},{21,13},{10,18... | collective-permute-start | bytes 1376264 | tf_op jit(solution)/shard_map/ppermute | solution.py:293
  125.1 20.1 %collective-permute-start.21 = (bf16[128,1792]{1,0:T(8,128)(2,1)S(1)}, bf16[128,1792]{1,0:T(8,128)(2,1)S(1)}, u32[]{:S(2)}, u32[]{:S(2)}) collective-permute-start(bf16[128,1792]{1,0:T(8,128)(2,1)S(1)} %shard_map.46), channel_id=1, source_target_pairs={{0,8},{4,12},{24,16},{28,20},{1,9},{5,13},{25,17},{29,21},{2,10},{... | collective-permute-start | bytes 1376264 | tf_op jit(solution)/shard_map/ppermute | solution.py:293
  127.1 37.7 %collective-permute-start.4 = (bf16[256,1792]{1,0:T(8,128)(2,1)S(1)}, bf16[256,1792]{1,0:T(8,128)(2,1)S(1)}, u32[]{:S(2)}, u32[]{:S(2)}) collective-permute-start(bf16[256,1792]{1,0:T(8,128)(2,1)S(1)} %shard_map.37), channel_id=1, source_target_pairs={{0,8},{4,12},{24,16},{28,20},{1,9},{5,13},{25,17},{29,21},{2,10},{... | collective-permute-start | bytes 2752520 | tf_op jit(solution)/shard_map/ppermute | solution.py:293
  129.2 53.0 %collective-permute-start.12 = (bf16[256,1792]{1,0:T(8,128)(2,1)S(1)}, bf16[256,1792]{1,0:T(8,128)(2,1)S(1)}, u32[]{:S(2)}, u32[]{:S(2)}) collective-permute-start(bf16[256,1792]{1,0:T(8,128)(2,1)S(1)} %shard_map.41), channel_id=1, source_target_pairs={{0,8},{4,12},{24,16},{28,20},{1,9},{5,13},{25,17},{29,21},{2,10},{... | collective-permute-start | bytes 2752520 | tf_op jit(solution)/shard_map/ppermute | solution.py:293
  146.7 36.9 %collective-permute-start.33 = (bf16[128,1792]{1,0:T(8,128)(2,1)S(1)}, bf16[128,1792]{1,0:T(8,128)(2,1)S(1)}, u32[]{:S(2)}, u32[]{:S(2)}) collective-permute-start(bf16[128,1792]{1,0:T(8,128)(2,1)S(1)} %shard_map.53.near), channel_id=1, source_target_pairs={{8,0},{12,4},{16,24},{20,28},{9,1},{13,5},{17,25},{21,29},{10,2},{... | collective-permute-start | bytes 1376264 | tf_op jit(solution)/shard_map/ppermute | solution.py:293
  148.0 35.6 %collective-permute-start.34 = (bf16[128,1792]{1,0:T(8,128)(2,1)S(1)}, bf16[128,1792]{1,0:T(8,128)(2,1)S(1)}, u32[]{:S(2)}, u32[]{:S(2)}) collective-permute-start(bf16[128,1792]{1,0:T(8,128)(2,1)S(1)} %collective-permute-done.32.away), channel_id=1, source_target_pairs={{8,0},{12,4},{16,24},{20,28},{9,1},{13,5},{17,25},{21,29},{10,2},{... | collective-permute-start | bytes 1376264 | tf_op jit(solution)/shard_map/ppermute | solution.py:293
  150.1 36.1 %collective-permute-start.23 = (bf16[128,1792]{1,0:T(8,128)(2,1)S(1)}, bf16[128,1792]{1,0:T(8,128)(2,1)S(1)}, u32[]{:S(2)}, u32[]{:S(2)}) collective-permute-start(bf16[128,1792]{1,0:T(8,128)(2,1)S(1)} %shard_map.48.near), channel_id=1, source_target_pairs={{8,16},{12,20},{16,8},{20,12},{9,17},{13,21},{17,9},{21,13},{10,18... | collective-permute-start | bytes 1376264 | tf_op jit(solution)/shard_map/ppermute | solution.py:293
  165.6 21.9 %collective-permute-start.5 = (bf16[128,1792]{1,0:T(8,128)(2,1)S(1)}, bf16[128,1792]{1,0:T(8,128)(2,1)S(1)}, u32[]{:S(2)}, u32[]{:S(2)}) collective-permute-start(bf16[128,1792]{1,0:T(8,128)(2,1)S(1)} %get-tuple-element.48), channel_id=1, source_target_pairs={{8,16},{12,20},{16,8},{20,12},{9,17},{13,21},{17,9},{21,13},{10,18... | collective-permute-start | bytes 1376264 | tf_op jit(solution)/shard_map/ppermute | solution.py:293
  184.3 31.0 %collective-permute-start.35 = (bf16[256,1792]{1,0:T(8,128)(2,1)S(1)}, bf16[256,1792]{1,0:T(8,128)(2,1)S(1)}, u32[]{:S(2)}, u32[]{:S(2)}) collective-permute-start(bf16[256,1792]{1,0:T(8,128)(2,1)S(1)} %shard_map.54.lo), channel_id=1, source_target_pairs={{0,4},{4,0},{8,12},{12,8},{16,20},{20,16},{24,28},{28,24},{1,5},{5... | collective-permute-start | bytes 2752520 | tf_op jit(solution)/shard_map/ppermute | solution.py:17
  184.9 17.9 %collective-permute-start.24 = (bf16[128,1792]{1,0:T(8,128)(2,1)S(1)}, bf16[128,1792]{1,0:T(8,128)(2,1)S(1)}, u32[]{:S(2)}, u32[]{:S(2)}) collective-permute-start(bf16[128,1792]{1,0:T(8,128)(2,1)S(1)} %shard_map.48.near), channel_id=1, source_target_pairs={{8,0},{12,4},{16,24},{20,28},{9,1},{13,5},{17,25},{21,29},{10,2},{... | collective-permute-start | bytes 1376264 | tf_op jit(solution)/shard_map/ppermute | solution.py:293
  186.2 23.0 %collective-permute-start.25 = (bf16[128,1792]{1,0:T(8,128)(2,1)S(1)}, bf16[128,1792]{1,0:T(8,128)(2,1)S(1)}, u32[]{:S(2)}, u32[]{:S(2)}) collective-permute-start(bf16[128,1792]{1,0:T(8,128)(2,1)S(1)} %collective-permute-done.23.away), channel_id=1, source_target_pairs={{8,0},{12,4},{16,24},{20,28},{9,1},{13,5},{17,25},{21,29},{10,2},{... | collective-permute-start | bytes 1376264 | tf_op jit(solution)/shard_map/ppermute | solution.py:293
  188.3 24.4 %collective-permute-start.7 = (bf16[128,1792]{1,0:T(8,128)(2,1)S(1)}, bf16[128,1792]{1,0:T(8,128)(2,1)S(1)}, u32[]{:S(2)}, u32[]{:S(2)}) collective-permute-start(bf16[128,1792]{1,0:T(8,128)(2,1)S(1)} %shard_map.39.near), channel_id=1, source_target_pairs={{8,16},{12,20},{16,8},{20,12},{9,17},{13,21},{17,9},{21,13},{10,18... | collective-permute-start | bytes 1376264 | tf_op jit(solution)/shard_map/ppermute | solution.py:293
  189.7 24.3 %collective-permute-start.14 = (bf16[128,1792]{1,0:T(8,128)(2,1)S(1)}, bf16[128,1792]{1,0:T(8,128)(2,1)S(1)}, u32[]{:S(2)}, u32[]{:S(2)}) collective-permute-start(bf16[128,1792]{1,0:T(8,128)(2,1)S(1)} %shard_map.43.near), channel_id=1, source_target_pairs={{8,16},{12,20},{16,8},{20,12},{9,17},{13,21},{17,9},{21,13},{10,18... | collective-permute-start | bytes 1376264 | tf_op jit(solution)/shard_map/ppermute | solution.py:293
  209.8 43.0 %collective-permute-start.26 = (bf16[256,1792]{1,0:T(8,128)(2,1)S(1)}, bf16[256,1792]{1,0:T(8,128)(2,1)S(1)}, u32[]{:S(2)}, u32[]{:S(2)}) collective-permute-start(bf16[256,1792]{1,0:T(8,128)(2,1)S(1)} %shard_map.49.lo), channel_id=1, source_target_pairs={{0,4},{4,0},{8,12},{12,8},{16,20},{20,16},{24,28},{28,24},{1,5},{5... | collective-permute-start | bytes 2752520 | tf_op jit(solution)/shard_map/ppermute | solution.py:17
  211.4 17.0 %collective-permute-start.8 = (bf16[128,1792]{1,0:T(8,128)(2,1)S(1)}, bf16[128,1792]{1,0:T(8,128)(2,1)S(1)}, u32[]{:S(2)}, u32[]{:S(2)}) collective-permute-start(bf16[128,1792]{1,0:T(8,128)(2,1)S(1)} %shard_map.39.near), channel_id=1, source_target_pairs={{8,0},{12,4},{16,24},{20,28},{9,1},{13,5},{17,25},{21,29},{10,2},{... | collective-permute-start | bytes 1376264 | tf_op jit(solution)/shard_map/ppermute | solution.py:293
  212.7 34.9 %collective-permute-start.15 = (bf16[128,1792]{1,0:T(8,128)(2,1)S(1)}, bf16[128,1792]{1,0:T(8,128)(2,1)S(1)}, u32[]{:S(2)}, u32[]{:S(2)}) collective-permute-start(bf16[128,1792]{1,0:T(8,128)(2,1)S(1)} %shard_map.43.near), channel_id=1, source_target_pairs={{8,0},{12,4},{16,24},{20,28},{9,1},{13,5},{17,25},{21,29},{10,2},{... | collective-permute-start | bytes 1376264 | tf_op jit(solution)/shard_map/ppermute | solution.py:293
  214.0 32.3 %collective-permute-start.9 = (bf16[128,1792]{1,0:T(8,128)(2,1)S(1)}, bf16[128,1792]{1,0:T(8,128)(2,1)S(1)}, u32[]{:S(2)}, u32[]{:S(2)}) collective-permute-start(bf16[128,1792]{1,0:T(8,128)(2,1)S(1)} %collective-permute-done.7.away), channel_id=1, source_target_pairs={{8,0},{12,4},{16,24},{20,28},{9,1},{13,5},{17,25},{21,29},{10,2},{... | collective-permute-start | bytes 1376264 | tf_op jit(solution)/shard_map/ppermute | solution.py:293
  215.3 36.3 %collective-permute-start.16 = (bf16[128,1792]{1,0:T(8,128)(2,1)S(1)}, bf16[128,1792]{1,0:T(8,128)(2,1)S(1)}, u32[]{:S(2)}, u32[]{:S(2)}) collective-permute-start(bf16[128,1792]{1,0:T(8,128)(2,1)S(1)} %collective-permute-done.14.away), channel_id=1, source_target_pairs={{8,0},{12,4},{16,24},{20,28},{9,1},{13,5},{17,25},{21,29},{10,2},{... | collective-permute-start | bytes 1376264 | tf_op jit(solution)/shard_map/ppermute | solution.py:293
  247.0 29.0 %collective-permute-start.37 = (bf16[128,1792]{1,0:T(8,128)(2,1)S(1)}, bf16[128,1792]{1,0:T(8,128)(2,1)S(1)}, u32[]{:S(2)}, u32[]{:S(2)}) collective-permute-start(bf16[128,1792]{1,0:T(8,128)(2,1)S(1)} %get-tuple-element.77.lo), channel_id=1, source_target_pairs={{0,4},{4,0},{8,12},{12,8},{16,20},{20,16},{24,28},{28,24},{1,5},{5... | collective-permute-start | bytes 1376264 | tf_op jit(solution)/shard_map/ppermute | solution.py:17
  264.7 19.8 %collective-permute-start.17 = (bf16[128,1792]{1,0:T(8,128)(2,1)S(1)}, bf16[128,1792]{1,0:T(8,128)(2,1)S(1)}, u32[]{:S(2)}, u32[]{:S(2)}) collective-permute-start(bf16[128,1792]{1,0:T(8,128)(2,1)S(1)} %get-tuple-element.54.lo), channel_id=1, source_target_pairs={{0,4},{4,0},{8,12},{12,8},{16,20},{20,16},{24,28},{28,24},{1,5},{5... | collective-permute-start | bytes 1376264 | tf_op jit(solution)/shard_map/ppermute | solution.py:17
  284.4 21.4 %collective-permute-start.39 = (bf16[128,3584]{1,0:T(8,128)(2,1)S(1)}, bf16[128,3584]{1,0:T(8,128)(2,1)S(1)}, u32[]{:S(2)}, u32[]{:S(2)}) collective-permute-start(bf16[128,3584]{1,0:T(8,128)(2,1)S(1)} %get-tuple-element.84), channel_id=1, source_target_pairs={{0,1},{1,0},{2,3},{3,2},{4,5},{5,4},{6,7},{7,6},{8,9},{9,8},{10,11... | collective-permute-start | bytes 2752520 | tf_op jit(solution)/shard_map/ppermute | solution.py:17
  306.8 22.8 %collective-permute-start.40 = (bf16[128,3584]{1,0:T(8,128)(2,1)S(1)}, bf16[128,3584]{1,0:T(8,128)(2,1)S(1)}, u32[]{:S(2)}, u32[]{:S(2)}) collective-permute-start(bf16[128,3584]{1,0:T(8,128)(2,1)S(1)} %shard_map.55), channel_id=1, source_target_pairs={{0,2},{1,3},{2,0},{3,1},{4,6},{5,7},{6,4},{7,5},{8,10},{9,11},{10,... | collective-permute-start | bytes 2752520 | tf_op jit(solution)/shard_map/ppermute | solution.py:17
  (12 other events, 123.1 us)
where the time goes:
time: 332 us; the launch traced here: 331 us
  waiting for transfers between devices  156 us (47%)
  Pallas kernels  128 us (39%)
  starting transfers between devices  45.3 us (14%)
    ppermute x23, waiting for transfers between devices, send(): return lax.ppermute(x, 'row', pairs)  86.4 us
    ppermute x18, waiting for transfers between devices, swap(): return lax.ppermute(x, axis, [(d, d ^ 1 << bit) for d in range(size)])  70 us
    pallas_call x6, Pallas kernels, back(): pl.pallas_call(functools.partial(back_body, bits, block, len(before) > 0)...  56.8 us
    pallas_call x6, Pallas kernels, rotate(): pl.pallas_call(functools.partial(rotate_body, bits, block, len(shards)),...  55.5 us
    ppermute x23, starting transfers between devices, send(): return lax.ppermute(x, 'row', pairs)  29.8 us
    ppermute x18, starting transfers between devices, swap(): return lax.ppermute(x, axis, [(d, d ^ 1 << bit) for d in range(size)])  15.5 us
    pallas_call x20, Pallas kernels, columns(): pl.pallas_call(body, grid_spec=pltpu.PrefetchScalarGridSpec(num_scalar_pr...  15.5 us
  transfers between devices with their start and end apart: 41, of which 15 were waited for; matrix products, arithmetic and copies ran while one was open for 0% of the time, Pallas kernels for 38%

commit v1 on v0

--- a/solution.py
+++ b/solution.py
@@ -97,105 +97,142 @@
             to[pl.ds(slot * rows, rows), :] = source[pl.ds(at, rows), :]
 
 
-def rotate_body(bits, block, n, idx, *refs):
-    shards, (b, away, keep, rows) = refs[:n], refs[n:]
+DEPTH = 4
+
+
+def stream(steps, fetch, work):
+    def prime(_=None):
+        for i in range(min(DEPTH - 1, steps)):
+            fetch(i, i).start()
+
+    def loop():
+        def step(i, carry):
+            slot = lax.rem(i, DEPTH)
+            fetch(i, slot).wait()
+
+            @pl.when(i + DEPTH - 1 < steps)
+            def _():
+                fetch(i + DEPTH - 1, lax.rem(i + DEPTH - 1, DEPTH)).start()
+
+            work(i, slot)
+            return carry
+
+        lax.fori_loop(0, steps, step, 0)
+
+    return prime, loop
+
+
+def rotate_body(bits, block, n, start, tile, idx, *refs):
+    shards, (b, away, keep, rows, ring, sems) = refs[:n], refs[n:]
     slots = 1 << len(bits)
-
-    @pl.when(pl.program_id(0) == 0)
-    def _():
-        for slot in range(slots):
-            p = {bit: slot >> (len(bits) - 1 - j) & 1 for j, bit in enumerate(bits)}
-            which = idx[1] ^ p[1]
-            if 2 in p:
-                which = which + 2 * (idx[2] ^ p[2])
-            copy_block(shards, which, idx[0] ^ p[0], block, rows, slot)
-
-    out = jnp.dot(rows[...], b[...], preferred_element_type=F32)
     half = slots // 2 * block
-    keep[...] = out[:half]
-    away[...] = out[half:].astype(BF16)
-
-
-def fixed(shape):
-    return pl.BlockSpec(shape, lambda i, idx: (0, 0), pipeline_mode=pl.Buffered(1))
+
+    def fetch(i, slot):
+        at = pl.multiple_of(start + i * tile, LANES)
+        return pltpu.make_async_copy(b.at[:, pl.ds(at, tile)], ring.at[slot], sems.at[slot])
+
+    def work(i, slot):
+        out = jnp.dot(rows[...], ring[slot], preferred_element_type=F32)
+        at = pl.ds(pl.multiple_of(i * tile, LANES), tile)
+        keep[:, at] = out[:half]
+        away[:, at] = out[half:].astype(BF16)
+
+    prime, loop = stream(keep.shape[1] // tile, fetch, work)
+    prime()
+    for slot in range(slots):
+        p = {bit: slot >> (len(bits) - 1 - j) & 1 for j, bit in enumerate(bits)}
+        which = idx[1] ^ p[1]
+        if 2 in p:
+            which = which + 2 * (idx[2] ^ p[2])
+        copy_block(shards, which, idx[0] ^ p[0], block, rows, slot)
+    loop()
+
+
+VMEM = pl.BlockSpec(memory_space=pltpu.VMEM)
+
+
+def kernel(body, outs, scratch, aliases, flops, moved, limit, idx, basis_at, *args):
+    specs = [pl.BlockSpec(memory_space=pltpu.SMEM)] + [VMEM] * len(args)
+    specs[1 + basis_at] = pl.BlockSpec(memory_space=pl.ANY)
+    return pl.pallas_call(
+        body,
+        in_specs=specs,
+        out_specs=[VMEM] * len(outs),
+        out_shape=outs,
+        scratch_shapes=scratch + [pltpu.SemaphoreType.DMA((DEPTH,))],
+        input_output_aliases=aliases,
+        compiler_params=pltpu.CompilerParams(vmem_limit_bytes=limit),
+        cost_estimate=pl.CostEstimate(flops=flops, bytes_accessed=moved, transcendentals=0),
+    )(idx, *args)
 
 
 def rotate(idx, shards, basis, start, w, bits, block):
     k = shards[0].shape[1]
-    tile = tile_of(w, 896)
-    first = start // tile
+    tile = tile_of(w, 256)
     count = block << len(bits)
-    rows = pl.BlockSpec((count // 2, tile), lambda i, idx: (0, i))
-    return pl.pallas_call(
-        functools.partial(rotate_body, bits, block, len(shards)),
-        grid_spec=pltpu.PrefetchScalarGridSpec(
-            num_scalar_prefetch=1,
-            grid=(w // tile,),
-            in_specs=[fixed(x.shape) for x in shards]
-            + [pl.BlockSpec((k, tile), lambda i, idx: (0, i + first))],
-            out_specs=[rows, rows],
-            scratch_shapes=[pltpu.VMEM((count, k), BF16)],
-        ),
-        out_shape=[
-            jax.ShapeDtypeStruct((count // 2, w), BF16),
-            jax.ShapeDtypeStruct((count // 2, w), F32),
-        ],
-        compiler_params=pltpu.CompilerParams(vmem_limit_bytes=30 << 20),
-        cost_estimate=pl.CostEstimate(
-            flops=2 * count * k * w, bytes_accessed=2 * k * w, transcendentals=0
-        ),
-        name="rotate",
-    )(idx, *shards, basis)
-
-
-def back_body(bits, block, more, idx, lo, hi, b, *refs):
+    return kernel(
+        functools.partial(rotate_body, bits, block, len(shards), start, tile),
+        [jax.ShapeDtypeStruct((count // 2, w), x) for x in (BF16, F32)],
+        [pltpu.VMEM((count, k), BF16), pltpu.VMEM((DEPTH, k, tile), BF16)],
+        {},
+        2 * count * k * w,
+        2 * k * w,
+        26 << 20,
+        idx,
+        len(shards),
+        *shards,
+        basis,
+    )
+
+
+def back_body(bits, block, more, start, tile, idx, lo, hi, b, *refs):
     parts = 1 << len(bits) - 1
-    rows, outs, before = refs[-1], refs[-1 - parts : -1], refs[:parts]
-
-    @pl.when(pl.program_id(0) == 0)
-    def _():
-        for slot in range(2 * parts):
-            p = {bit: idx[bit] ^ (slot >> bit & 1) for bit in bits}
-            at = p[bits[1]] if len(bits) == 2 else 2 * p[bits[1]] + p[bits[2]]
-            copy_block((lo, hi), p[bits[0]], at, block, rows, slot)
-
-    out = lax.dot_general(rows[...], b[...], ALONG, preferred_element_type=F32)
-    for n in range(parts):
-        part = out[2 * n * block : 2 * (n + 1) * block]
-        if more:
-            part = part + before[n][...]
-        outs[n][...] = part.astype(outs[n].dtype)
+    before = refs[:parts]
+    outs, (rows, ring, sems) = refs[-3 - parts : -3], refs[-3:]
+    w = lo.shape[1]
+
+    def fetch(i, slot):
+        at = pl.ds(pl.multiple_of(i * tile, tile), tile)
+        return pltpu.make_async_copy(b.at[at, pl.ds(start, w)], ring.at[slot], sems.at[slot])
+
+    def work(i, slot):
+        out = lax.dot_general(rows[...], ring[slot], ALONG, preferred_element_type=F32)
+        at = pl.ds(pl.multiple_of(i * tile, LANES), tile)
+        for n in range(parts):
+            part = out[2 * n * block : 2 * (n + 1) * block]
+            if more:
+                part = part + before[n][:, at]
+            outs[n][:, at] = part.astype(outs[n].dtype)
+
+    prime, loop = stream(b.shape[0] // tile, fetch, work)
+    prime()
+    for slot in range(2 * parts):
+        p = {bit: idx[bit] ^ (slot >> bit & 1) for bit in bits}
+        at = p[bits[1]] if len(bits) == 2 else 2 * p[bits[1]] + p[bits[2]]
+        copy_block((lo, hi), p[bits[0]], at, block, rows, slot)
+    loop()
 
 
 def back(idx, lo, hi, basis, start, w, bits, block, before, last):
     k = basis.shape[0]
-    tile = tile_of(k, 896)
-    rows = pl.BlockSpec((2 * block, tile), lambda i, idx: (0, i))
+    tile = tile_of(k, 512)
     parts = 1 << len(bits) - 1
-    return pl.pallas_call(
-        functools.partial(back_body, bits, block, len(before) > 0),
-        grid_spec=pltpu.PrefetchScalarGridSpec(
-            num_scalar_prefetch=1,
-            grid=(k // tile,),
-            in_specs=[
-                fixed(lo.shape),
-                fixed(hi.shape),
-                pl.BlockSpec((tile, w), lambda i, idx: (i, start // w)),
-            ]
-            + [rows] * len(before),
-            out_specs=[rows] * parts,
-            scratch_shapes=[pltpu.VMEM((2 * lo.shape[0], w), BF16)],
-        ),
-        out_shape=[
-            jax.ShapeDtypeStruct((2 * block, k), BF16 if last and n % 2 else F32)
-            for n in range(parts)
-        ],
-        compiler_params=pltpu.CompilerParams(vmem_limit_bytes=24 << 20),
-        cost_estimate=pl.CostEstimate(
-            flops=4 * lo.shape[0] * k * w, bytes_accessed=2 * k * w, transcendentals=0
-        ),
-        name="back",
-    )(idx, lo, hi, basis, *before)
+    kinds = [BF16 if last and n % 2 else F32 for n in range(parts)]
+    return kernel(
+        functools.partial(back_body, bits, block, len(before) > 0, start, tile),
+        [jax.ShapeDtypeStruct((2 * block, k), x) for x in kinds],
+        [pltpu.VMEM((2 * lo.shape[0], w), BF16), pltpu.VMEM((DEPTH, tile, w), BF16)],
+        {4 + n: n for n in range(len(before)) if kinds[n] == F32},
+        4 * lo.shape[0] * k * w,
+        2 * k * w,
+        26 << 20,
+        idx,
+        2,
+        lo,
+        hi,
+        basis,
+        *before,
+    )
 
 
 def columns(body, idx, ins, outs):
@@ -282,7 +319,11 @@
     bits = [r & 1, c & 1, ((r >> 2) ^ (c >> 1)) & 1, (r >> 1) & 1, ((r >> 2) ^ (r >> 1)) & 1]
     idx = jnp.stack(bits).astype(jnp.int32)
     block = eigen.shape[0]
-    w = eigen.shape[1] // len(chunks)
+    starts, at = [], 0
+    for part, _, _ in chunks:
+        starts.append(at)
+        at += eigen.shape[1] * part // PARTS
+    widths = [b - a for a, b in zip(starts, starts[1:] + [at])]
     s = jax.ShapeDtypeStruct
     mid = [d for d in range(n_row) if (d >> 2 ^ d >> 1) & 1]
     inwards = [(d ^ 2, d) for d in mid]
@@ -300,7 +341,7 @@
 
     def cols(body, ins, outs):
         ins = [x if isinstance(x, tuple) else (x, 0) for x in ins]
-        outs = [s((rows, w), kind) for rows, kind in outs]
+        outs = [s((rows, ins[0][0].shape[1]), kind) for rows, kind in outs]
         out = columns(body, idx, ins, outs)
         return out if len(outs) > 1 else out[0]
 
@@ -308,27 +349,27 @@
     shards = {"own": (gradient, col(gradient, 0)), "far": (far_half, col(far_half, 0))}
     other = send(eigen, inwards)
 
-    def rotated(held, start, order):
-        away, keep = rotate(idx, held, basis, start, w, order, block)
+    def rotated(held, i, order):
+        away, keep = rotate(idx, held, basis, starts[i], widths[i], order, block)
         got = row(away)
         total = cols(sum_body, [keep, got], [(keep.shape[0], BF16)])
         return [keep, got, send(total, inwards)]
 
     held = {}
     halves = [(2 * block, F32), (2 * block, BF16)]
-    for i, (cut, _) in enumerate(chunks):
+    for i, (_, cut, _) in enumerate(chunks):
         if cut:
-            part = rotated(shards["own"], i * w, (0, 1))
-            part += rotated(shards["far"], i * w, (0, 1))
+            part = rotated(shards["own"], i, (0, 1))
+            part += rotated(shards["far"], i, (0, 1))
             keep, away = cols(merge_body, part, halves)
         else:
-            part = rotated(shards["own"] + shards["far"], i * w, (0, 2, 1))
+            part = rotated(shards["own"] + shards["far"], i, (0, 2, 1))
             keep, away = cols(halve_body, part, halves)
         got = send(away, across)
-        held[i] = cols(scale_body, [keep, got, (eigen, i * w), (other, i * w)], halves[1:])
+        held[i] = cols(scale_body, [keep, got, (eigen, starts[i]), (other, starts[i])], halves[1:])
 
     done = ()
-    for i, (_, cut) in enumerate(chunks):
+    for i, (_, _, cut) in enumerate(chunks):
         near = held[i]
         away = send(near, across)
         near_out = send(near, outwards)
@@ -337,13 +378,13 @@
         if not cut:
             lo = cols(join_body, parts, [(4 * block, BF16)])
             hi = row(lo)
-            done = back(idx, lo, hi, basis, i * w, w, (0, 2, 1), block, done, last)
+            done = back(idx, lo, hi, basis, starts[i], widths[i], (0, 2, 1), block, done, last)
             continue
         own, far = cols(part_body, parts, [(2 * block, BF16)] * 2)
         parts = []
         for lo, before in ((own, done[:2]), (far, done[2:])):
             hi = row(lo)
-            parts += back(idx, lo, hi, basis, i * w, w, (0, 1), block, before, last)
+            parts += back(idx, lo, hi, basis, starts[i], widths[i], (0, 1), block, before, last)
         done = tuple(parts)
 
     def final(body, ins):
@@ -356,11 +397,12 @@
 
 
 CHUNKS = (
-    (True, False),
-    (True, False),
-    (False, True),
-    (False, True),
+    (7, True, False),
+    (7, True, False),
+    (7, False, True),
+    (7, False, True),
 )
+PARTS = sum(part for part, _, _ in CHUNKS)
 
 
 def solution(mesh):

time: 332 us -> 324 us (0.976)
  Pallas kernels: 128 us -> 109 us
  waiting for transfers between devices: 156 us -> 163 us
    pallas_call x12, Pallas kernels: 112 us -> 93.8 us  [kernel(): pl.pallas_call(body, in_specs=specs, out_specs=[VMEM] * len(outs), out_sh...]
    ppermute x23, waiting for transfers between devices: 86.4 us -> 91.8 us  [send(): return lax.ppermute(x, 'row', pairs)]
    ppermute x23, starting transfers between devices: 29.8 us -> 33.3 us  [send(): return lax.ppermute(x, 'row', pairs)]
  transfers between devices with their start and end apart: 41 -> 41, of which waited for: 15 -> 16; matrix products, arithmetic and copies ran while one was open for 0% -> 0% of each run, Pallas kernels for 38% -> 33%
where the time goes in v1:
time: 324 us; the launch traced here: 323 us
  waiting for transfers between devices  163 us (50%)
  Pallas kernels  109 us (34%)
  starting transfers between devices  48.5 us (15%)
    pallas_call x12, Pallas kernels, kernel(): pl.pallas_call(body, in_specs=specs, out_specs=[VMEM] * len(outs), out_sh...  93.8 us
    ppermute x23, waiting for transfers between devices, send(): return lax.ppermute(x, 'row', pairs)  91.8 us
    ppermute x18, waiting for transfers between devices, swap(): return lax.ppermute(x, axis, [(d, d ^ 1 << bit) for d in range(size)])  71.6 us
    ppermute x23, starting transfers between devices, send(): return lax.ppermute(x, 'row', pairs)  33.3 us
    pallas_call x20, Pallas kernels, columns(): pl.pallas_call(body, grid_spec=pltpu.PrefetchScalarGridSpec(num_scalar_pr...  15.5 us
    ppermute x18, starting transfers between devices, swap(): return lax.ppermute(x, axis, [(d, d ^ 1 << bit) for d in range(size)])  15.2 us
  transfers between devices with their start and end apart: 41, of which 16 were waited for; matrix products, arithmetic and copies ran while one was open for 0% of the time, Pallas kernels for 33%

profile of v1, /device:TPU:0, one launch (start us, length us, event | category | flops | bytes accessed | tf_op | source)
XLA Modules:
  0.0 323.2 jit_solution(10306038344230599453)
XLA Ops:
  0.0 3.0 collective-permute-start.1
  3.0 20.6 %collective-permute-done.1.refs_2_.refs_0_ = bf16[128,3584]{1,0:T(8,128)(2,1)S(1)} collective-permute-done((bf16[128,3584]{1,0:T(8,128)(2,1)}, bf16[128,3584]{1,0:T(8,128)(2,1)S(1)}, u32[]{:S(2)}, u32[]{:S(2)}) %collective-permute-start.1) | collective-permute-done | bytes 917536 | tf_op jit(solution)/shard_map/ppermute | solution.py:17
  24.9 6.6 %shard_map.54 = (bf16[128,1792]{1,0:T(8,128)(2,1)S(1)}, f32[128,1792]{1,0:T(8,128)S(1)}) custom-call(s32[5]{0:T(128)S(1)} %stack.23.idx, bf16[128,3584]{1,0:T(8,128)(2,1)S(1)} %copy-done.1, bf16[128,3584]{1,0:T(8,128)(2,1)S(1)} %collective-permute-done.refs_1_, bf16[3584,7168]{1,0:T(8,128)(2,1)} %b.11), custom_call_target="tpu_custom_call" | custom-call | flops 3288334336 | bytes 12845056 | tf_op jit(solution)/shard_map/pallas_call | solution.py:157
  33.4 3.6 %collective-permute-start.6 = (f32[64,7168]{1,0:T(8,128)S(1)}, f32[64,7168]{1,0:T(8,128)S(1)}, u32[]{:S(2)}, u32[]{:S(2)}) collective-permute-start(f32[64,7168]{1,0:T(8,128)S(1)} %copy-done), channel_id=1, source_target_pairs={{0,8},{4,12},{24,16},{28,20},{1,9},{5,13},{25,17},{29,21},{2,10},{... | collective-permute-start | bytes 5505032 | tf_op jit(solution)/shard_map/ppermute | solution.py:334
  37.0 6.6 %shard_map.47 = (bf16[128,1792]{1,0:T(8,128)(2,1)S(1)}, f32[128,1792]{1,0:T(8,128)S(1)}) custom-call(s32[5]{0:T(128)S(1)} %stack.23.idx, bf16[128,3584]{1,0:T(8,128)(2,1)S(1)} %copy-done.1, bf16[128,3584]{1,0:T(8,128)(2,1)S(1)} %collective-permute-done.refs_1_, bf16[3584,7168]{1,0:T(8,128)(2,1)} %b.11), custom_call_target="tpu_custom_call" | custom-call | flops 3288334336 | bytes 12845056 | tf_op jit(solution)/shard_map/pallas_call | solution.py:157
  45.2 4.3 %collective-permute-start.28 = (bf16[128,1792]{1,0:T(8,128)(2,1)S(1)}, bf16[128,1792]{1,0:T(8,128)(2,1)S(1)}, u32[]{:S(2)}, u32[]{:S(2)}) collective-permute-start(bf16[128,1792]{1,0:T(8,128)(2,1)S(1)} %shard_map.55), channel_id=1, source_target_pairs={{0,8},{4,12},{24,16},{28,20},{1,9},{5,13},{25,17},{29,21},{2,10},{... | collective-permute-start | bytes 1376264 | tf_op jit(solution)/shard_map/ppermute | solution.py:334
  49.5 6.6 %shard_map.56 = (bf16[128,1792]{1,0:T(8,128)(2,1)S(1)}, f32[128,1792]{1,0:T(8,128)S(1)}) custom-call(s32[5]{0:T(128)S(1)} %stack.23.idx, bf16[128,3584]{1,0:T(8,128)(2,1)S(1)} %collective-permute-done.1.refs_2_.refs_0_, bf16[128,3584]{1,0:T(8,128)(2,1)S(1)} %collective-permute-done.2.refs_3_.refs_1_, bf16[3584,7168]{1,0:T(8,128)(2,1)} %b.11), custom_call_target="tpu_custom_call" | custom-call | flops 3288334336 | bytes 12845056 | tf_op jit(solution)/shard_map/pallas_call | solution.py:157
  57.8 9.9 %shard_map.37 = (bf16[256,1792]{1,0:T(8,128)(2,1)S(1)}, f32[256,1792]{1,0:T(8,128)S(1)}) custom-call(s32[5]{0:T(128)S(1)} %stack.23.idx, bf16[128,3584]{1,0:T(8,128)(2,1)S(1)} %copy-done.2, bf16[128,3584]{1,0:T(8,128)(2,1)S(1)} %collective-permute-done.refs_1_, bf16[128,3584]{1,0:T(8,128)(2,1)S(1)} %collective-permute-done.1.refs_2_.refs_0_, ...), custom_call_target="tpu_custom_call" | custom-call | flops 6576668672 | bytes 12845056 | tf_op jit(solution)/shard_map/pallas_call | solution.py:157
  70.2 9.9 %shard_map.42 = (bf16[256,1792]{1,0:T(8,128)(2,1)S(1)}, f32[256,1792]{1,0:T(8,128)S(1)}) custom-call(s32[5]{0:T(128)S(1)} %stack.23.idx, bf16[128,3584]{1,0:T(8,128)(2,1)S(1)} %copy-done.2, bf16[128,3584]{1,0:T(8,128)(2,1)S(1)} %collective-permute-done.refs_1_, bf16[128,3584]{1,0:T(8,128)(2,1)S(1)} %collective-permute-done.1.refs_2_.refs_0_, ...), custom_call_target="tpu_custom_call" | custom-call | flops 6576668672 | bytes 12845056 | tf_op jit(solution)/shard_map/pallas_call | solution.py:157
  80.1 6.9 %collective-permute-done.28.own_e = bf16[128,1792]{1,0:T(8,128)(2,1)S(1)} collective-permute-done((bf16[128,1792]{1,0:T(8,128)(2,1)S(1)}, bf16[128,1792]{1,0:T(8,128)(2,1)S(1)}, u32[]{:S(2)}, u32[]{:S(2)}) %collective-permute-start.28) | collective-permute-done | bytes 458784 | tf_op jit(solution)/shard_map/ppermute | solution.py:334
  87.6 6.6 %shard_map.49 = (bf16[128,1792]{1,0:T(8,128)(2,1)S(1)}, f32[128,1792]{1,0:T(8,128)S(1)}) custom-call(s32[5]{0:T(128)S(1)} %stack.23.idx, bf16[128,3584]{1,0:T(8,128)(2,1)S(1)} %collective-permute-done.1.refs_2_.refs_0_, bf16[128,3584]{1,0:T(8,128)(2,1)S(1)} %collective-permute-done.2.refs_3_.refs_1_, bf16[3584,7168]{1,0:T(8,128)(2,1)} %b.11), custom_call_target="tpu_custom_call" | custom-call | flops 3288334336 | bytes 12845056 | tf_op jit(solution)/shard_map/pallas_call | solution.py:157
  94.2 2.0 collective-permute-done.30.far_e
  98.9 19.2 %collective-permute-done.20.got.far_y = bf16[128,1792]{1,0:T(8,128)(2,1)S(1)} collective-permute-done((bf16[128,1792]{1,0:T(8,128)(2,1)S(1)}, bf16[128,1792]{1,0:T(8,128)(2,1)S(1)}, u32[]{:S(2)}, u32[]{:S(2)}) %collective-permute-start.20) | collective-permute-done | bytes 458784 | tf_op jit(solution)/shard_map/ppermute | solution.py:17
  118.1 4.1 %collective-permute-start.19 = (bf16[128,1792]{1,0:T(8,128)(2,1)S(1)}, bf16[128,1792]{1,0:T(8,128)(2,1)S(1)}, u32[]{:S(2)}, u32[]{:S(2)}) collective-permute-start(bf16[128,1792]{1,0:T(8,128)(2,1)S(1)} %shard_map.48), channel_id=1, source_target_pairs={{0,8},{4,12},{24,16},{28,20},{1,9},{5,13},{25,17},{29,21},{2,10},{... | collective-permute-start | bytes 1376264 | tf_op jit(solution)/shard_map/ppermute | solution.py:334
  129.7 3.3 %collective-permute-done.19.own_e = bf16[128,1792]{1,0:T(8,128)(2,1)S(1)} collective-permute-done((bf16[128,1792]{1,0:T(8,128)(2,1)S(1)}, bf16[128,1792]{1,0:T(8,128)(2,1)S(1)}, u32[]{:S(2)}, u32[]{:S(2)}) %collective-permute-start.19) | collective-permute-done | bytes 458784 | tf_op jit(solution)/shard_map/ppermute | solution.py:334
  133.1 9.8 %collective-permute-done.21.far_e = bf16[128,1792]{1,0:T(8,128)(2,1)S(1)} collective-permute-done((bf16[128,1792]{1,0:T(8,128)(2,1)S(1)}, bf16[128,1792]{1,0:T(8,128)(2,1)S(1)}, u32[]{:S(2)}, u32[]{:S(2)}) %collective-permute-start.21) | collective-permute-done | bytes 458784 | tf_op jit(solution)/shard_map/ppermute | solution.py:334
  148.5 14.0 %collective-permute-done.4.more = bf16[256,1792]{1,0:T(8,128)(2,1)S(1)} collective-permute-done((bf16[256,1792]{1,0:T(8,128)(2,1)S(1)}, bf16[256,1792]{1,0:T(8,128)(2,1)S(1)}, u32[]{:S(2)}, u32[]{:S(2)}) %collective-permute-start.4) | collective-permute-done | bytes 917536 | tf_op jit(solution)/shard_map/ppermute | solution.py:334
  164.1 15.0 %collective-permute-done.12.more = bf16[256,1792]{1,0:T(8,128)(2,1)S(1)} collective-permute-done((bf16[256,1792]{1,0:T(8,128)(2,1)S(1)}, bf16[256,1792]{1,0:T(8,128)(2,1)S(1)}, u32[]{:S(2)}, u32[]{:S(2)}) %collective-permute-start.12) | collective-permute-done | bytes 917536 | tf_op jit(solution)/shard_map/ppermute | solution.py:334
  187.4 12.4 %collective-permute-done.24.near_out = bf16[128,1792]{1,0:T(8,128)(2,1)S(1)} collective-permute-done((bf16[128,1792]{1,0:T(8,128)(2,1)S(1)}, bf16[128,1792]{1,0:T(8,128)(2,1)S(1)}, u32[]{:S(2)}, u32[]{:S(2)}) %collective-permute-start.24) | collective-permute-done | bytes 458784 | tf_op jit(solution)/shard_map/ppermute | solution.py:334
  199.9 5.5 %collective-permute-done.25.away_out = bf16[128,1792]{1,0:T(8,128)(2,1)S(1)} collective-permute-done((bf16[128,1792]{1,0:T(8,128)(2,1)S(1)}, bf16[128,1792]{1,0:T(8,128)(2,1)S(1)}, u32[]{:S(2)}, u32[]{:S(2)}) %collective-permute-start.25) | collective-permute-done | bytes 458784 | tf_op jit(solution)/shard_map/ppermute | solution.py:334
  212.8 10.1 %shard_map.61 = (f32[128,3584]{1,0:T(8,128)S(1)}, f32[128,3584]{1,0:T(8,128)S(1)}, f32[128,3584]{1,0:T(8,128)S(1)}, f32[128,3584]{1,0:T(8,128)S(1)}) custom-call(s32[5]{0:T(128)S(1)} %stack.23.idx, bf16[256,1792]{1,0:T(8,128)(2,1)S(1)} %shard_map.60.lo, bf16[256,1792]{1,0:T(8,128)(2,1)S(1)} %collective-permute-done.35.hi, bf16[3584,7168]{1,0:T(8,128)(2,1)} %b.11), custom_call_target="tpu_custom_call" | custom-call | flops 6576668672 | bytes 12845056 | tf_op jit(solution)/shard_map/pallas_call | solution.py:157
  222.9 19.1 %collective-permute-done.9.away_out = bf16[128,1792]{1,0:T(8,128)(2,1)S(1)} collective-permute-done((bf16[128,1792]{1,0:T(8,128)(2,1)S(1)}, bf16[128,1792]{1,0:T(8,128)(2,1)S(1)}, u32[]{:S(2)}, u32[]{:S(2)}) %collective-permute-start.9) | collective-permute-done | bytes 458784 | tf_op jit(solution)/shard_map/ppermute | solution.py:334
  243.2 3.7 %collective-permute-done.16.away_out = bf16[128,1792]{1,0:T(8,128)(2,1)S(1)} collective-permute-done((bf16[128,1792]{1,0:T(8,128)(2,1)S(1)}, bf16[128,1792]{1,0:T(8,128)(2,1)S(1)}, u32[]{:S(2)}, u32[]{:S(2)}) %collective-permute-start.16) | collective-permute-done | bytes 458784 | tf_op jit(solution)/shard_map/ppermute | solution.py:334
  248.1 10.1 %shard_map.62 = (f32[128,3584]{1,0:T(8,128)S(1)}, f32[128,3584]{1,0:T(8,128)S(1)}, f32[128,3584]{1,0:T(8,128)S(1)}, f32[128,3584]{1,0:T(8,128)S(1)}) custom-call(s32[5]{0:T(128)S(1)} %stack.23.idx, bf16[256,1792]{1,0:T(8,128)(2,1)S(1)} %shard_map.53.lo, ...), custom_call_target="tpu_custom_call", output_to_operand_aliasing={{0}: (4, {}), {1}: (5, {}), {2}: (6, {}), {3}: (7, {})} | custom-call | flops 6576668672 | bytes 12845056 | tf_op jit(solution)/shard_map/pallas_call | solution.py:157
  259.8 4.1 %collective-permute-done.38.hi = bf16[128,1792]{1,0:T(8,128)(2,1)S(1)} collective-permute-done((bf16[128,1792]{1,0:T(8,128)(2,1)S(1)}, bf16[128,1792]{1,0:T(8,128)(2,1)S(1)}, u32[]{:S(2)}, u32[]{:S(2)}) %collective-permute-start.38) | collective-permute-done | bytes 458784 | tf_op jit(solution)/shard_map/ppermute | solution.py:17
  263.9 6.8 %shard_map.65 = (f32[128,3584]{1,0:T(8,128)S(1)}, f32[128,3584]{1,0:T(8,128)S(1)}) custom-call(s32[5]{0:T(128)S(1)} %stack.23.idx, bf16[128,1792]{1,0:T(8,128)(2,1)S(1)} %get-tuple-element.78.lo, bf16[128,1792]{1,0:T(8,128)(2,1)S(1)} %collective-permute-done.38.hi, bf16[3584,7168]{1,0:T(8,128)(2,1)} %b.11, ...), custom_call_target="tpu_custom_call", output_to_operand_aliasing={{0}: (4, {}), {1}: (5, {})} | custom-call | flops 3288334336 | bytes 12845056 | tf_op jit(solution)/shard_map/pallas_call | solution.py:157
  270.7 6.8 %shard_map.66 = (f32[128,3584]{1,0:T(8,128)S(1)}, bf16[128,3584]{1,0:T(8,128)(2,1)S(1)}) custom-call(s32[5]{0:T(128)S(1)} %stack.23.idx, bf16[128,1792]{1,0:T(8,128)(2,1)S(1)} %get-tuple-element.77.lo, bf16[128,1792]{1,0:T(8,128)(2,1)S(1)} %collective-permute-done.37.hi, bf16[3584,7168]{1,0:T(8,128)(2,1)} %b.11, ...), custom_call_target="tpu_custom_call", output_to_operand_aliasing={{0}: (4, {})} | custom-call | flops 3288334336 | bytes 12845056 | tf_op jit(solution)/shard_map/pallas_call | solution.py:157
  277.7 6.8 %shard_map.63 = (f32[128,3584]{1,0:T(8,128)S(1)}, f32[128,3584]{1,0:T(8,128)S(1)}) custom-call(s32[5]{0:T(128)S(1)} %stack.23.idx, bf16[128,1792]{1,0:T(8,128)(2,1)S(1)} %get-tuple-element.54.lo, bf16[128,1792]{1,0:T(8,128)(2,1)S(1)} %collective-permute-done.17.hi, bf16[3584,7168]{1,0:T(8,128)(2,1)} %b.11, ...), custom_call_target="tpu_custom_call", output_to_operand_aliasing={{0}: (4, {}), {1}: (5, {})} | custom-call | flops 3288334336 | bytes 12845056 | tf_op jit(solution)/shard_map/pallas_call | solution.py:157
  284.6 6.0 %collective-permute-done.10.hi = bf16[128,1792]{1,0:T(8,128)(2,1)S(1)} collective-permute-done((bf16[128,1792]{1,0:T(8,128)(2,1)S(1)}, bf16[128,1792]{1,0:T(8,128)(2,1)S(1)}, u32[]{:S(2)}, u32[]{:S(2)}) %collective-permute-start.10) | collective-permute-done | bytes 458784 | tf_op jit(solution)/shard_map/ppermute | solution.py:17
  290.6 6.8 %shard_map.64 = (f32[128,3584]{1,0:T(8,128)S(1)}, bf16[128,3584]{1,0:T(8,128)(2,1)S(1)}) custom-call(s32[5]{0:T(128)S(1)} %stack.23.idx, bf16[128,1792]{1,0:T(8,128)(2,1)S(1)} %get-tuple-element.49.lo, bf16[128,1792]{1,0:T(8,128)(2,1)S(1)} %collective-permute-done.10.hi, bf16[3584,7168]{1,0:T(8,128)(2,1)} %b.11, ...), custom_call_target="tpu_custom_call", output_to_operand_aliasing={{0}: (4, {})} | custom-call | flops 3288334336 | bytes 12845056 | tf_op jit(solution)/shard_map/pallas_call | solution.py:157
  300.1 21.3 %collective-permute-done.40.far = bf16[128,3584]{1,0:T(8,128)(2,1)S(1)} collective-permute-done((bf16[128,3584]{1,0:T(8,128)(2,1)S(1)}, bf16[128,3584]{1,0:T(8,128)(2,1)S(1)}, u32[]{:S(2)}, u32[]{:S(2)}) %collective-permute-start.40) | collective-permute-done | bytes 917536 | tf_op jit(solution)/shard_map/ppermute | solution.py:17
  321.3 1.9 shard_map.68
  (89 shorter events, 49.1 us)
Async XLA Ops:
  0.0 23.5 %collective-permute-start.1 = (bf16[128,3584]{1,0:T(8,128)(2,1)}, bf16[128,3584]{1,0:T(8,128)(2,1)S(1)}, u32[]{:S(2)}, u32[]{:S(2)}) collective-permute-start(bf16[128,3584]{1,0:T(8,128)(2,1)} %refs_0_.7), channel_id=1, source_target_pairs={{0,2},{1,3},{2,0},{3,1},{4,6},{5,7},{6,4},{7,5},{8,10},{9,11},{10,... | collective-permute-start | bytes 2752520 | tf_op jit(solution)/shard_map/ppermute | solution.py:17
  3.0 20.6 %collective-permute-start = (bf16[128,3584]{1,0:T(8,128)(2,1)}, bf16[128,3584]{1,0:T(8,128)(2,1)S(1)}, u32[]{:S(2)}, u32[]{:S(2)}) collective-permute-start(bf16[128,3584]{1,0:T(8,128)(2,1)} %refs_0_.7), channel_id=1, source_target_pairs={{0,1},{1,0},{2,3},{3,2},{4,5},{5,4},{6,7},{7,6},{8,9},{9,8},{10,11... | collective-permute-start | bytes 2752520 | tf_op jit(solution)/shard_map/ppermute | solution.py:17
  23.5 26.0 %collective-permute-start.2 = (bf16[128,3584]{1,0:T(8,128)(2,1)S(1)}, bf16[128,3584]{1,0:T(8,128)(2,1)S(1)}, u32[]{:S(2)}, u32[]{:S(2)}) collective-permute-start(bf16[128,3584]{1,0:T(8,128)(2,1)S(1)} %collective-permute-done.1.refs_2_.refs_0_), channel_id=1, source_target_pairs={{0,1},{1,0},{2,3},{3,2},{4,5},{5,4},{6,7},{7,6},{8,9},{9,8},{10,11... | collective-permute-start | bytes 2752520 | tf_op jit(solution)/shard_map/ppermute | solution.py:17
  33.4 93.6 %collective-permute-start.6 = (f32[64,7168]{1,0:T(8,128)S(1)}, f32[64,7168]{1,0:T(8,128)S(1)}, u32[]{:S(2)}, u32[]{:S(2)}) collective-permute-start(f32[64,7168]{1,0:T(8,128)S(1)} %copy-done), channel_id=1, source_target_pairs={{0,8},{4,12},{24,16},{28,20},{1,9},{5,13},{25,17},{29,21},{2,10},{... | collective-permute-start | bytes 5505032 | tf_op jit(solution)/shard_map/ppermute | solution.py:334
  43.6 54.0 %collective-permute-start.18 = (bf16[128,1792]{1,0:T(8,128)(2,1)S(1)}, bf16[128,1792]{1,0:T(8,128)(2,1)S(1)}, u32[]{:S(2)}, u32[]{:S(2)}) collective-permute-start(bf16[128,1792]{1,0:T(8,128)(2,1)S(1)} %get-tuple-element.56), channel_id=1, source_target_pairs={{0,4},{4,0},{8,12},{12,8},{16,20},{20,16},{24,28},{28,24},{1,5},{5... | collective-permute-start | bytes 1376264 | tf_op jit(solution)/shard_map/ppermute | solution.py:17
  45.2 41.9 %collective-permute-start.28 = (bf16[128,1792]{1,0:T(8,128)(2,1)S(1)}, bf16[128,1792]{1,0:T(8,128)(2,1)S(1)}, u32[]{:S(2)}, u32[]{:S(2)}) collective-permute-start(bf16[128,1792]{1,0:T(8,128)(2,1)S(1)} %shard_map.55), channel_id=1, source_target_pairs={{0,8},{4,12},{24,16},{28,20},{1,9},{5,13},{25,17},{29,21},{2,10},{... | collective-permute-start | bytes 1376264 | tf_op jit(solution)/shard_map/ppermute | solution.py:334
  67.7 55.2 %collective-permute-start.3 = (bf16[256,1792]{1,0:T(8,128)(2,1)S(1)}, bf16[256,1792]{1,0:T(8,128)(2,1)S(1)}, u32[]{:S(2)}, u32[]{:S(2)}) collective-permute-start(bf16[256,1792]{1,0:T(8,128)(2,1)S(1)} %get-tuple-element.46), channel_id=1, source_target_pairs={{0,4},{4,0},{8,12},{12,8},{16,20},{20,16},{24,28},{28,24},{1,5},{5... | collective-permute-start | bytes 2752520 | tf_op jit(solution)/shard_map/ppermute | solution.py:17
  68.9 27.3 %collective-permute-start.30 = (bf16[128,1792]{1,0:T(8,128)(2,1)S(1)}, bf16[128,1792]{1,0:T(8,128)(2,1)S(1)}, u32[]{:S(2)}, u32[]{:S(2)}) collective-permute-start(bf16[128,1792]{1,0:T(8,128)(2,1)S(1)} %shard_map.57), channel_id=1, source_target_pairs={{0,8},{4,12},{24,16},{28,20},{1,9},{5,13},{25,17},{29,21},{2,10},{... | collective-permute-start | bytes 1376264 | tf_op jit(solution)/shard_map/ppermute | solution.py:334
  87.1 37.8 %collective-permute-start.11 = (bf16[256,1792]{1,0:T(8,128)(2,1)S(1)}, bf16[256,1792]{1,0:T(8,128)(2,1)S(1)}, u32[]{:S(2)}, u32[]{:S(2)}) collective-permute-start(bf16[256,1792]{1,0:T(8,128)(2,1)S(1)} %get-tuple-element.51), channel_id=1, source_target_pairs={{0,4},{4,0},{8,12},{12,8},{16,20},{20,16},{24,28},{28,24},{1,5},{5... | collective-permute-start | bytes 2752520 | tf_op jit(solution)/shard_map/ppermute | solution.py:17
  96.2 21.9 %collective-permute-start.20 = (bf16[128,1792]{1,0:T(8,128)(2,1)S(1)}, bf16[128,1792]{1,0:T(8,128)(2,1)S(1)}, u32[]{:S(2)}, u32[]{:S(2)}) collective-permute-start(bf16[128,1792]{1,0:T(8,128)(2,1)S(1)} %get-tuple-element.58), channel_id=1, source_target_pairs={{0,4},{4,0},{8,12},{12,8},{16,20},{20,16},{24,28},{28,24},{1,5},{5... | collective-permute-start | bytes 1376264 | tf_op jit(solution)/shard_map/ppermute | solution.py:17
  97.6 30.7 %collective-permute-start.31 = (bf16[128,1792]{1,0:T(8,128)(2,1)S(1)}, bf16[128,1792]{1,0:T(8,128)(2,1)S(1)}, u32[]{:S(2)}, u32[]{:S(2)}) collective-permute-start(bf16[128,1792]{1,0:T(8,128)(2,1)S(1)} %get-tuple-element.66), channel_id=1, source_target_pairs={{8,16},{12,20},{16,8},{20,12},{9,17},{13,21},{17,9},{21,13},{10,18... | collective-permute-start | bytes 1376264 | tf_op jit(solution)/shard_map/ppermute | solution.py:334
  122.8 20.1 %collective-permute-start.21 = (bf16[128,1792]{1,0:T(8,128)(2,1)S(1)}, bf16[128,1792]{1,0:T(8,128)(2,1)S(1)}, u32[]{:S(2)}, u32[]{:S(2)}) collective-permute-start(bf16[128,1792]{1,0:T(8,128)(2,1)S(1)} %shard_map.50), channel_id=1, source_target_pairs={{0,8},{4,12},{24,16},{28,20},{1,9},{5,13},{25,17},{29,21},{2,10},{... | collective-permute-start | bytes 1376264 | tf_op jit(solution)/shard_map/ppermute | solution.py:334
  124.9 37.7 %collective-permute-start.4 = (bf16[256,1792]{1,0:T(8,128)(2,1)S(1)}, bf16[256,1792]{1,0:T(8,128)(2,1)S(1)}, u32[]{:S(2)}, u32[]{:S(2)}) collective-permute-start(bf16[256,1792]{1,0:T(8,128)(2,1)S(1)} %shard_map.38), channel_id=1, source_target_pairs={{0,8},{4,12},{24,16},{28,20},{1,9},{5,13},{25,17},{29,21},{2,10},{... | collective-permute-start | bytes 2752520 | tf_op jit(solution)/shard_map/ppermute | solution.py:334
  126.9 52.1 %collective-permute-start.12 = (bf16[256,1792]{1,0:T(8,128)(2,1)S(1)}, bf16[256,1792]{1,0:T(8,128)(2,1)S(1)}, u32[]{:S(2)}, u32[]{:S(2)}) collective-permute-start(bf16[256,1792]{1,0:T(8,128)(2,1)S(1)} %shard_map.43), channel_id=1, source_target_pairs={{0,8},{4,12},{24,16},{28,20},{1,9},{5,13},{25,17},{29,21},{2,10},{... | collective-permute-start | bytes 2752520 | tf_op jit(solution)/shard_map/ppermute | solution.py:334
  129.0 16.8 %collective-permute-start.32 = (bf16[128,1792]{1,0:T(8,128)(2,1)S(1)}, bf16[128,1792]{1,0:T(8,128)(2,1)S(1)}, u32[]{:S(2)}, u32[]{:S(2)}) collective-permute-start(bf16[128,1792]{1,0:T(8,128)(2,1)S(1)} %shard_map.59.near), channel_id=1, source_target_pairs={{8,16},{12,20},{16,8},{20,12},{9,17},{13,21},{17,9},{21,13},{10,18... | collective-permute-start | bytes 1376264 | tf_op jit(solution)/shard_map/ppermute | solution.py:334
  144.5 36.2 %collective-permute-start.33 = (bf16[128,1792]{1,0:T(8,128)(2,1)S(1)}, bf16[128,1792]{1,0:T(8,128)(2,1)S(1)}, u32[]{:S(2)}, u32[]{:S(2)}) collective-permute-start(bf16[128,1792]{1,0:T(8,128)(2,1)S(1)} %shard_map.59.near), channel_id=1, source_target_pairs={{8,0},{12,4},{16,24},{20,28},{9,1},{13,5},{17,25},{21,29},{10,2},{... | collective-permute-start | bytes 1376264 | tf_op jit(solution)/shard_map/ppermute | solution.py:334
  145.8 34.9 %collective-permute-start.34 = (bf16[128,1792]{1,0:T(8,128)(2,1)S(1)}, bf16[128,1792]{1,0:T(8,128)(2,1)S(1)}, u32[]{:S(2)}, u32[]{:S(2)}) collective-permute-start(bf16[128,1792]{1,0:T(8,128)(2,1)S(1)} %collective-permute-done.32.away), channel_id=1, source_target_pairs={{8,0},{12,4},{16,24},{20,28},{9,1},{13,5},{17,25},{21,29},{10,2},{... | collective-permute-start | bytes 1376264 | tf_op jit(solution)/shard_map/ppermute | solution.py:334
  147.8 35.4 %collective-permute-start.23 = (bf16[128,1792]{1,0:T(8,128)(2,1)S(1)}, bf16[128,1792]{1,0:T(8,128)(2,1)S(1)}, u32[]{:S(2)}, u32[]{:S(2)}) collective-permute-start(bf16[128,1792]{1,0:T(8,128)(2,1)S(1)} %shard_map.52.near), channel_id=1, source_target_pairs={{8,16},{12,20},{16,8},{20,12},{9,17},{13,21},{17,9},{21,13},{10,18... | collective-permute-start | bytes 1376264 | tf_op jit(solution)/shard_map/ppermute | solution.py:334
  163.4 21.2 %collective-permute-start.5 = (bf16[128,1792]{1,0:T(8,128)(2,1)S(1)}, bf16[128,1792]{1,0:T(8,128)(2,1)S(1)}, u32[]{:S(2)}, u32[]{:S(2)}) collective-permute-start(bf16[128,1792]{1,0:T(8,128)(2,1)S(1)} %get-tuple-element.48), channel_id=1, source_target_pairs={{8,16},{12,20},{16,8},{20,12},{9,17},{13,21},{17,9},{21,13},{10,18... | collective-permute-start | bytes 1376264 | tf_op jit(solution)/shard_map/ppermute | solution.py:334
  181.4 30.1 %collective-permute-start.35 = (bf16[256,1792]{1,0:T(8,128)(2,1)S(1)}, bf16[256,1792]{1,0:T(8,128)(2,1)S(1)}, u32[]{:S(2)}, u32[]{:S(2)}) collective-permute-start(bf16[256,1792]{1,0:T(8,128)(2,1)S(1)} %shard_map.60.lo), channel_id=1, source_target_pairs={{0,4},{4,0},{8,12},{12,8},{16,20},{20,16},{24,28},{28,24},{1,5},{5... | collective-permute-start | bytes 2752520 | tf_op jit(solution)/shard_map/ppermute | solution.py:17
  181.9 17.9 %collective-permute-start.24 = (bf16[128,1792]{1,0:T(8,128)(2,1)S(1)}, bf16[128,1792]{1,0:T(8,128)(2,1)S(1)}, u32[]{:S(2)}, u32[]{:S(2)}) collective-permute-start(bf16[128,1792]{1,0:T(8,128)(2,1)S(1)} %shard_map.52.near), channel_id=1, source_target_pairs={{8,0},{12,4},{16,24},{20,28},{9,1},{13,5},{17,25},{21,29},{10,2},{... | collective-permute-start | bytes 1376264 | tf_op jit(solution)/shard_map/ppermute | solution.py:334
  183.2 22.1 %collective-permute-start.25 = (bf16[128,1792]{1,0:T(8,128)(2,1)S(1)}, bf16[128,1792]{1,0:T(8,128)(2,1)S(1)}, u32[]{:S(2)}, u32[]{:S(2)}) collective-permute-start(bf16[128,1792]{1,0:T(8,128)(2,1)S(1)} %collective-permute-done.23.away), channel_id=1, source_target_pairs={{8,0},{12,4},{16,24},{20,28},{9,1},{13,5},{17,25},{21,29},{10,2},{... | collective-permute-start | bytes 1376264 | tf_op jit(solution)/shard_map/ppermute | solution.py:334
  185.3 23.6 %collective-permute-start.7 = (bf16[128,1792]{1,0:T(8,128)(2,1)S(1)}, bf16[128,1792]{1,0:T(8,128)(2,1)S(1)}, u32[]{:S(2)}, u32[]{:S(2)}) collective-permute-start(bf16[128,1792]{1,0:T(8,128)(2,1)S(1)} %shard_map.40.near), channel_id=1, source_target_pairs={{8,16},{12,20},{16,8},{20,12},{9,17},{13,21},{17,9},{21,13},{10,18... | collective-permute-start | bytes 1376264 | tf_op jit(solution)/shard_map/ppermute | solution.py:334
  186.7 23.5 %collective-permute-start.14 = (bf16[128,1792]{1,0:T(8,128)(2,1)S(1)}, bf16[128,1792]{1,0:T(8,128)(2,1)S(1)}, u32[]{:S(2)}, u32[]{:S(2)}) collective-permute-start(bf16[128,1792]{1,0:T(8,128)(2,1)S(1)} %shard_map.45.near), channel_id=1, source_target_pairs={{8,16},{12,20},{16,8},{20,12},{9,17},{13,21},{17,9},{21,13},{10,18... | collective-permute-start | bytes 1376264 | tf_op jit(solution)/shard_map/ppermute | solution.py:334
  206.0 42.1 %collective-permute-start.26 = (bf16[256,1792]{1,0:T(8,128)(2,1)S(1)}, bf16[256,1792]{1,0:T(8,128)(2,1)S(1)}, u32[]{:S(2)}, u32[]{:S(2)}) collective-permute-start(bf16[256,1792]{1,0:T(8,128)(2,1)S(1)} %shard_map.53.lo), channel_id=1, source_target_pairs={{0,4},{4,0},{8,12},{12,8},{16,20},{20,16},{24,28},{28,24},{1,5},{5... | collective-permute-start | bytes 2752520 | tf_op jit(solution)/shard_map/ppermute | solution.py:17
  208.9 34.3 %collective-permute-start.15 = (bf16[128,1792]{1,0:T(8,128)(2,1)S(1)}, bf16[128,1792]{1,0:T(8,128)(2,1)S(1)}, u32[]{:S(2)}, u32[]{:S(2)}) collective-permute-start(bf16[128,1792]{1,0:T(8,128)(2,1)S(1)} %shard_map.45.near), channel_id=1, source_target_pairs={{8,0},{12,4},{16,24},{20,28},{9,1},{13,5},{17,25},{21,29},{10,2},{... | collective-permute-start | bytes 1376264 | tf_op jit(solution)/shard_map/ppermute | solution.py:334
  210.2 31.8 %collective-permute-start.9 = (bf16[128,1792]{1,0:T(8,128)(2,1)S(1)}, bf16[128,1792]{1,0:T(8,128)(2,1)S(1)}, u32[]{:S(2)}, u32[]{:S(2)}) collective-permute-start(bf16[128,1792]{1,0:T(8,128)(2,1)S(1)} %collective-permute-done.7.away), channel_id=1, source_target_pairs={{8,0},{12,4},{16,24},{20,28},{9,1},{13,5},{17,25},{21,29},{10,2},{... | collective-permute-start | bytes 1376264 | tf_op jit(solution)/shard_map/ppermute | solution.py:334
  211.5 35.4 %collective-permute-start.16 = (bf16[128,1792]{1,0:T(8,128)(2,1)S(1)}, bf16[128,1792]{1,0:T(8,128)(2,1)S(1)}, u32[]{:S(2)}, u32[]{:S(2)}) collective-permute-start(bf16[128,1792]{1,0:T(8,128)(2,1)S(1)} %collective-permute-done.14.away), channel_id=1, source_target_pairs={{8,0},{12,4},{16,24},{20,28},{9,1},{13,5},{17,25},{21,29},{10,2},{... | collective-permute-start | bytes 1376264 | tf_op jit(solution)/shard_map/ppermute | solution.py:334
  242.6 28.1 %collective-permute-start.37 = (bf16[128,1792]{1,0:T(8,128)(2,1)S(1)}, bf16[128,1792]{1,0:T(8,128)(2,1)S(1)}, u32[]{:S(2)}, u32[]{:S(2)}) collective-permute-start(bf16[128,1792]{1,0:T(8,128)(2,1)S(1)} %get-tuple-element.77.lo), channel_id=1, source_target_pairs={{0,4},{4,0},{8,12},{12,8},{16,20},{20,16},{24,28},{28,24},{1,5},{5... | collective-permute-start | bytes 1376264 | tf_op jit(solution)/shard_map/ppermute | solution.py:17
  258.2 19.5 %collective-permute-start.17 = (bf16[128,1792]{1,0:T(8,128)(2,1)S(1)}, bf16[128,1792]{1,0:T(8,128)(2,1)S(1)}, u32[]{:S(2)}, u32[]{:S(2)}) collective-permute-start(bf16[128,1792]{1,0:T(8,128)(2,1)S(1)} %get-tuple-element.54.lo), channel_id=1, source_target_pairs={{0,4},{4,0},{8,12},{12,8},{16,20},{20,16},{24,28},{28,24},{1,5},{5... | collective-permute-start | bytes 1376264 | tf_op jit(solution)/shard_map/ppermute | solution.py:17
  277.6 19.9 %collective-permute-start.39 = (bf16[128,3584]{1,0:T(8,128)(2,1)S(1)}, bf16[128,3584]{1,0:T(8,128)(2,1)S(1)}, u32[]{:S(2)}, u32[]{:S(2)}) collective-permute-start(bf16[128,3584]{1,0:T(8,128)(2,1)S(1)} %get-tuple-element.84), channel_id=1, source_target_pairs={{0,1},{1,0},{2,3},{3,2},{4,5},{5,4},{6,7},{7,6},{8,9},{9,8},{10,11... | collective-permute-start | bytes 2752520 | tf_op jit(solution)/shard_map/ppermute | solution.py:17
  298.5 22.8 %collective-permute-start.40 = (bf16[128,3584]{1,0:T(8,128)(2,1)S(1)}, bf16[128,3584]{1,0:T(8,128)(2,1)S(1)}, u32[]{:S(2)}, u32[]{:S(2)}) collective-permute-start(bf16[128,3584]{1,0:T(8,128)(2,1)S(1)} %shard_map.67), channel_id=1, source_target_pairs={{0,2},{1,3},{2,0},{3,1},{4,6},{5,7},{6,4},{7,5},{8,10},{9,11},{10,... | collective-permute-start | bytes 2752520 | tf_op jit(solution)/shard_map/ppermute | solution.py:17
  (12 other events, 120.4 us)

commit v2 on v1

--- a/solution.py
+++ b/solution.py
@@ -397,10 +397,10 @@
 
 
 CHUNKS = (
-    (7, True, False),
-    (7, True, False),
-    (7, False, True),
-    (7, False, True),
+    (1, True, False),
+    (1, True, False),
+    (1, False, True),
+    (1, False, True),
 )
 PARTS = sum(part for part, _, _ in CHUNKS)
 

time: 324 us -> 324 us (level)
  no operation moved by 1% of the time
where the time goes in v2:
time: 324 us; the launch traced here: 323 us
  waiting for transfers between devices  163 us (50%)
  Pallas kernels  109 us (34%)
  starting transfers between devices  48.5 us (15%)
    pallas_call x12, Pallas kernels, kernel(): pl.pallas_call(body, in_specs=specs, out_specs=[VMEM] * len(outs), out_sh...  93.8 us
    ppermute x23, waiting for transfers between devices, send(): return lax.ppermute(x, 'row', pairs)  91.8 us
    ppermute x18, waiting for transfers between devices, swap(): return lax.ppermute(x, axis, [(d, d ^ 1 << bit) for d in range(size)])  71.6 us
    ppermute x23, starting transfers between devices, send(): return lax.ppermute(x, 'row', pairs)  33.3 us
    pallas_call x20, Pallas kernels, columns(): pl.pallas_call(body, grid_spec=pltpu.PrefetchScalarGridSpec(num_scalar_pr...  15.5 us
    ppermute x18, starting transfers between devices, swap(): return lax.ppermute(x, axis, [(d, d ^ 1 << bit) for d in range(size)])  15.2 us
  transfers between devices with their start and end apart: 41, of which 16 were waited for; matrix products, arithmetic and copies ran while one was open for 0% of the time, Pallas kernels for 33%

profile of v2, /device:TPU:0, one launch (start us, length us, event | category | flops | bytes accessed | tf_op | source)
XLA Modules:
  0.0 323.2 jit_solution(10306038344230599453)
XLA Ops:
  0.0 3.0 collective-permute-start.1
  3.0 20.6 %collective-permute-done.1.refs_2_.refs_0_ = bf16[128,3584]{1,0:T(8,128)(2,1)S(1)} collective-permute-done((bf16[128,3584]{1,0:T(8,128)(2,1)}, bf16[128,3584]{1,0:T(8,128)(2,1)S(1)}, u32[]{:S(2)}, u32[]{:S(2)}) %collective-permute-start.1) | collective-permute-done | bytes 917536 | tf_op jit(solution)/shard_map/ppermute | solution.py:17
  24.9 6.6 %shard_map.54 = (bf16[128,1792]{1,0:T(8,128)(2,1)S(1)}, f32[128,1792]{1,0:T(8,128)S(1)}) custom-call(s32[5]{0:T(128)S(1)} %stack.23.idx, bf16[128,3584]{1,0:T(8,128)(2,1)S(1)} %copy-done.1, bf16[128,3584]{1,0:T(8,128)(2,1)S(1)} %collective-permute-done.refs_1_, bf16[3584,7168]{1,0:T(8,128)(2,1)} %b.11), custom_call_target="tpu_custom_call" | custom-call | flops 3288334336 | bytes 12845056 | tf_op jit(solution)/shard_map/pallas_call | solution.py:157
  33.4 3.6 %collective-permute-start.6 = (f32[64,7168]{1,0:T(8,128)S(1)}, f32[64,7168]{1,0:T(8,128)S(1)}, u32[]{:S(2)}, u32[]{:S(2)}) collective-permute-start(f32[64,7168]{1,0:T(8,128)S(1)} %copy-done), channel_id=1, source_target_pairs={{0,8},{4,12},{24,16},{28,20},{1,9},{5,13},{25,17},{29,21},{2,10},{... | collective-permute-start | bytes 5505032 | tf_op jit(solution)/shard_map/ppermute | solution.py:334
  37.0 6.6 %shard_map.47 = (bf16[128,1792]{1,0:T(8,128)(2,1)S(1)}, f32[128,1792]{1,0:T(8,128)S(1)}) custom-call(s32[5]{0:T(128)S(1)} %stack.23.idx, bf16[128,3584]{1,0:T(8,128)(2,1)S(1)} %copy-done.1, bf16[128,3584]{1,0:T(8,128)(2,1)S(1)} %collective-permute-done.refs_1_, bf16[3584,7168]{1,0:T(8,128)(2,1)} %b.11), custom_call_target="tpu_custom_call" | custom-call | flops 3288334336 | bytes 12845056 | tf_op jit(solution)/shard_map/pallas_call | solution.py:157
  45.2 4.3 %collective-permute-start.28 = (bf16[128,1792]{1,0:T(8,128)(2,1)S(1)}, bf16[128,1792]{1,0:T(8,128)(2,1)S(1)}, u32[]{:S(2)}, u32[]{:S(2)}) collective-permute-start(bf16[128,1792]{1,0:T(8,128)(2,1)S(1)} %shard_map.55), channel_id=1, source_target_pairs={{0,8},{4,12},{24,16},{28,20},{1,9},{5,13},{25,17},{29,21},{2,10},{... | collective-permute-start | bytes 1376264 | tf_op jit(solution)/shard_map/ppermute | solution.py:334
  49.5 6.6 %shard_map.56 = (bf16[128,1792]{1,0:T(8,128)(2,1)S(1)}, f32[128,1792]{1,0:T(8,128)S(1)}) custom-call(s32[5]{0:T(128)S(1)} %stack.23.idx, bf16[128,3584]{1,0:T(8,128)(2,1)S(1)} %collective-permute-done.1.refs_2_.refs_0_, bf16[128,3584]{1,0:T(8,128)(2,1)S(1)} %collective-permute-done.2.refs_3_.refs_1_, bf16[3584,7168]{1,0:T(8,128)(2,1)} %b.11), custom_call_target="tpu_custom_call" | custom-call | flops 3288334336 | bytes 12845056 | tf_op jit(solution)/shard_map/pallas_call | solution.py:157
  57.8 9.9 %shard_map.37 = (bf16[256,1792]{1,0:T(8,128)(2,1)S(1)}, f32[256,1792]{1,0:T(8,128)S(1)}) custom-call(s32[5]{0:T(128)S(1)} %stack.23.idx, bf16[128,3584]{1,0:T(8,128)(2,1)S(1)} %copy-done.2, bf16[128,3584]{1,0:T(8,128)(2,1)S(1)} %collective-permute-done.refs_1_, bf16[128,3584]{1,0:T(8,128)(2,1)S(1)} %collective-permute-done.1.refs_2_.refs_0_, ...), custom_call_target="tpu_custom_call" | custom-call | flops 6576668672 | bytes 12845056 | tf_op jit(solution)/shard_map/pallas_call | solution.py:157
  70.2 9.9 %shard_map.42 = (bf16[256,1792]{1,0:T(8,128)(2,1)S(1)}, f32[256,1792]{1,0:T(8,128)S(1)}) custom-call(s32[5]{0:T(128)S(1)} %stack.23.idx, bf16[128,3584]{1,0:T(8,128)(2,1)S(1)} %copy-done.2, bf16[128,3584]{1,0:T(8,128)(2,1)S(1)} %collective-permute-done.refs_1_, bf16[128,3584]{1,0:T(8,128)(2,1)S(1)} %collective-permute-done.1.refs_2_.refs_0_, ...), custom_call_target="tpu_custom_call" | custom-call | flops 6576668672 | bytes 12845056 | tf_op jit(solution)/shard_map/pallas_call | solution.py:157
  80.1 6.9 %collective-permute-done.28.own_e = bf16[128,1792]{1,0:T(8,128)(2,1)S(1)} collective-permute-done((bf16[128,1792]{1,0:T(8,128)(2,1)S(1)}, bf16[128,1792]{1,0:T(8,128)(2,1)S(1)}, u32[]{:S(2)}, u32[]{:S(2)}) %collective-permute-start.28) | collective-permute-done | bytes 458784 | tf_op jit(solution)/shard_map/ppermute | solution.py:334
  87.6 6.6 %shard_map.49 = (bf16[128,1792]{1,0:T(8,128)(2,1)S(1)}, f32[128,1792]{1,0:T(8,128)S(1)}) custom-call(s32[5]{0:T(128)S(1)} %stack.23.idx, bf16[128,3584]{1,0:T(8,128)(2,1)S(1)} %collective-permute-done.1.refs_2_.refs_0_, bf16[128,3584]{1,0:T(8,128)(2,1)S(1)} %collective-permute-done.2.refs_3_.refs_1_, bf16[3584,7168]{1,0:T(8,128)(2,1)} %b.11), custom_call_target="tpu_custom_call" | custom-call | flops 3288334336 | bytes 12845056 | tf_op jit(solution)/shard_map/pallas_call | solution.py:157
  94.2 2.0 collective-permute-done.30.far_e
  98.9 19.2 %collective-permute-done.20.got.far_y = bf16[128,1792]{1,0:T(8,128)(2,1)S(1)} collective-permute-done((bf16[128,1792]{1,0:T(8,128)(2,1)S(1)}, bf16[128,1792]{1,0:T(8,128)(2,1)S(1)}, u32[]{:S(2)}, u32[]{:S(2)}) %collective-permute-start.20) | collective-permute-done | bytes 458784 | tf_op jit(solution)/shard_map/ppermute | solution.py:17
  118.1 4.1 %collective-permute-start.19 = (bf16[128,1792]{1,0:T(8,128)(2,1)S(1)}, bf16[128,1792]{1,0:T(8,128)(2,1)S(1)}, u32[]{:S(2)}, u32[]{:S(2)}) collective-permute-start(bf16[128,1792]{1,0:T(8,128)(2,1)S(1)} %shard_map.48), channel_id=1, source_target_pairs={{0,8},{4,12},{24,16},{28,20},{1,9},{5,13},{25,17},{29,21},{2,10},{... | collective-permute-start | bytes 1376264 | tf_op jit(solution)/shard_map/ppermute | solution.py:334
  129.7 3.3 %collective-permute-done.19.own_e = bf16[128,1792]{1,0:T(8,128)(2,1)S(1)} collective-permute-done((bf16[128,1792]{1,0:T(8,128)(2,1)S(1)}, bf16[128,1792]{1,0:T(8,128)(2,1)S(1)}, u32[]{:S(2)}, u32[]{:S(2)}) %collective-permute-start.19) | collective-permute-done | bytes 458784 | tf_op jit(solution)/shard_map/ppermute | solution.py:334
  133.1 9.8 %collective-permute-done.21.far_e = bf16[128,1792]{1,0:T(8,128)(2,1)S(1)} collective-permute-done((bf16[128,1792]{1,0:T(8,128)(2,1)S(1)}, bf16[128,1792]{1,0:T(8,128)(2,1)S(1)}, u32[]{:S(2)}, u32[]{:S(2)}) %collective-permute-start.21) | collective-permute-done | bytes 458784 | tf_op jit(solution)/shard_map/ppermute | solution.py:334
  148.5 14.0 %collective-permute-done.4.more = bf16[256,1792]{1,0:T(8,128)(2,1)S(1)} collective-permute-done((bf16[256,1792]{1,0:T(8,128)(2,1)S(1)}, bf16[256,1792]{1,0:T(8,128)(2,1)S(1)}, u32[]{:S(2)}, u32[]{:S(2)}) %collective-permute-start.4) | collective-permute-done | bytes 917536 | tf_op jit(solution)/shard_map/ppermute | solution.py:334
  164.1 15.0 %collective-permute-done.12.more = bf16[256,1792]{1,0:T(8,128)(2,1)S(1)} collective-permute-done((bf16[256,1792]{1,0:T(8,128)(2,1)S(1)}, bf16[256,1792]{1,0:T(8,128)(2,1)S(1)}, u32[]{:S(2)}, u32[]{:S(2)}) %collective-permute-start.12) | collective-permute-done | bytes 917536 | tf_op jit(solution)/shard_map/ppermute | solution.py:334
  187.4 12.4 %collective-permute-done.24.near_out = bf16[128,1792]{1,0:T(8,128)(2,1)S(1)} collective-permute-done((bf16[128,1792]{1,0:T(8,128)(2,1)S(1)}, bf16[128,1792]{1,0:T(8,128)(2,1)S(1)}, u32[]{:S(2)}, u32[]{:S(2)}) %collective-permute-start.24) | collective-permute-done | bytes 458784 | tf_op jit(solution)/shard_map/ppermute | solution.py:334
  199.9 5.5 %collective-permute-done.25.away_out = bf16[128,1792]{1,0:T(8,128)(2,1)S(1)} collective-permute-done((bf16[128,1792]{1,0:T(8,128)(2,1)S(1)}, bf16[128,1792]{1,0:T(8,128)(2,1)S(1)}, u32[]{:S(2)}, u32[]{:S(2)}) %collective-permute-start.25) | collective-permute-done | bytes 458784 | tf_op jit(solution)/shard_map/ppermute | solution.py:334
  212.8 10.1 %shard_map.61 = (f32[128,3584]{1,0:T(8,128)S(1)}, f32[128,3584]{1,0:T(8,128)S(1)}, f32[128,3584]{1,0:T(8,128)S(1)}, f32[128,3584]{1,0:T(8,128)S(1)}) custom-call(s32[5]{0:T(128)S(1)} %stack.23.idx, bf16[256,1792]{1,0:T(8,128)(2,1)S(1)} %shard_map.60.lo, bf16[256,1792]{1,0:T(8,128)(2,1)S(1)} %collective-permute-done.35.hi, bf16[3584,7168]{1,0:T(8,128)(2,1)} %b.11), custom_call_target="tpu_custom_call" | custom-call | flops 6576668672 | bytes 12845056 | tf_op jit(solution)/shard_map/pallas_call | solution.py:157
  222.9 19.1 %collective-permute-done.9.away_out = bf16[128,1792]{1,0:T(8,128)(2,1)S(1)} collective-permute-done((bf16[128,1792]{1,0:T(8,128)(2,1)S(1)}, bf16[128,1792]{1,0:T(8,128)(2,1)S(1)}, u32[]{:S(2)}, u32[]{:S(2)}) %collective-permute-start.9) | collective-permute-done | bytes 458784 | tf_op jit(solution)/shard_map/ppermute | solution.py:334
  243.2 3.7 %collective-permute-done.16.away_out = bf16[128,1792]{1,0:T(8,128)(2,1)S(1)} collective-permute-done((bf16[128,1792]{1,0:T(8,128)(2,1)S(1)}, bf16[128,1792]{1,0:T(8,128)(2,1)S(1)}, u32[]{:S(2)}, u32[]{:S(2)}) %collective-permute-start.16) | collective-permute-done | bytes 458784 | tf_op jit(solution)/shard_map/ppermute | solution.py:334
  248.1 10.1 %shard_map.62 = (f32[128,3584]{1,0:T(8,128)S(1)}, f32[128,3584]{1,0:T(8,128)S(1)}, f32[128,3584]{1,0:T(8,128)S(1)}, f32[128,3584]{1,0:T(8,128)S(1)}) custom-call(s32[5]{0:T(128)S(1)} %stack.23.idx, bf16[256,1792]{1,0:T(8,128)(2,1)S(1)} %shard_map.53.lo, ...), custom_call_target="tpu_custom_call", output_to_operand_aliasing={{0}: (4, {}), {1}: (5, {}), {2}: (6, {}), {3}: (7, {})} | custom-call | flops 6576668672 | bytes 12845056 | tf_op jit(solution)/shard_map/pallas_call | solution.py:157
  259.8 4.1 %collective-permute-done.38.hi = bf16[128,1792]{1,0:T(8,128)(2,1)S(1)} collective-permute-done((bf16[128,1792]{1,0:T(8,128)(2,1)S(1)}, bf16[128,1792]{1,0:T(8,128)(2,1)S(1)}, u32[]{:S(2)}, u32[]{:S(2)}) %collective-permute-start.38) | collective-permute-done | bytes 458784 | tf_op jit(solution)/shard_map/ppermute | solution.py:17
  263.9 6.8 %shard_map.65 = (f32[128,3584]{1,0:T(8,128)S(1)}, f32[128,3584]{1,0:T(8,128)S(1)}) custom-call(s32[5]{0:T(128)S(1)} %stack.23.idx, bf16[128,1792]{1,0:T(8,128)(2,1)S(1)} %get-tuple-element.78.lo, bf16[128,1792]{1,0:T(8,128)(2,1)S(1)} %collective-permute-done.38.hi, bf16[3584,7168]{1,0:T(8,128)(2,1)} %b.11, ...), custom_call_target="tpu_custom_call", output_to_operand_aliasing={{0}: (4, {}), {1}: (5, {})} | custom-call | flops 3288334336 | bytes 12845056 | tf_op jit(solution)/shard_map/pallas_call | solution.py:157
  270.7 6.8 %shard_map.66 = (f32[128,3584]{1,0:T(8,128)S(1)}, bf16[128,3584]{1,0:T(8,128)(2,1)S(1)}) custom-call(s32[5]{0:T(128)S(1)} %stack.23.idx, bf16[128,1792]{1,0:T(8,128)(2,1)S(1)} %get-tuple-element.77.lo, bf16[128,1792]{1,0:T(8,128)(2,1)S(1)} %collective-permute-done.37.hi, bf16[3584,7168]{1,0:T(8,128)(2,1)} %b.11, ...), custom_call_target="tpu_custom_call", output_to_operand_aliasing={{0}: (4, {})} | custom-call | flops 3288334336 | bytes 12845056 | tf_op jit(solution)/shard_map/pallas_call | solution.py:157
  277.7 6.8 %shard_map.63 = (f32[128,3584]{1,0:T(8,128)S(1)}, f32[128,3584]{1,0:T(8,128)S(1)}) custom-call(s32[5]{0:T(128)S(1)} %stack.23.idx, bf16[128,1792]{1,0:T(8,128)(2,1)S(1)} %get-tuple-element.54.lo, bf16[128,1792]{1,0:T(8,128)(2,1)S(1)} %collective-permute-done.17.hi, bf16[3584,7168]{1,0:T(8,128)(2,1)} %b.11, ...), custom_call_target="tpu_custom_call", output_to_operand_aliasing={{0}: (4, {}), {1}: (5, {})} | custom-call | flops 3288334336 | bytes 12845056 | tf_op jit(solution)/shard_map/pallas_call | solution.py:157
  284.6 6.0 %collective-permute-done.10.hi = bf16[128,1792]{1,0:T(8,128)(2,1)S(1)} collective-permute-done((bf16[128,1792]{1,0:T(8,128)(2,1)S(1)}, bf16[128,1792]{1,0:T(8,128)(2,1)S(1)}, u32[]{:S(2)}, u32[]{:S(2)}) %collective-permute-start.10) | collective-permute-done | bytes 458784 | tf_op jit(solution)/shard_map/ppermute | solution.py:17
  290.6 6.8 %shard_map.64 = (f32[128,3584]{1,0:T(8,128)S(1)}, bf16[128,3584]{1,0:T(8,128)(2,1)S(1)}) custom-call(s32[5]{0:T(128)S(1)} %stack.23.idx, bf16[128,1792]{1,0:T(8,128)(2,1)S(1)} %get-tuple-element.49.lo, bf16[128,1792]{1,0:T(8,128)(2,1)S(1)} %collective-permute-done.10.hi, bf16[3584,7168]{1,0:T(8,128)(2,1)} %b.11, ...), custom_call_target="tpu_custom_call", output_to_operand_aliasing={{0}: (4, {})} | custom-call | flops 3288334336 | bytes 12845056 | tf_op jit(solution)/shard_map/pallas_call | solution.py:157
  300.1 21.3 %collective-permute-done.40.far = bf16[128,3584]{1,0:T(8,128)(2,1)S(1)} collective-permute-done((bf16[128,3584]{1,0:T(8,128)(2,1)S(1)}, bf16[128,3584]{1,0:T(8,128)(2,1)S(1)}, u32[]{:S(2)}, u32[]{:S(2)}) %collective-permute-start.40) | collective-permute-done | bytes 917536 | tf_op jit(solution)/shard_map/ppermute | solution.py:17
  321.3 1.9 shard_map.68
  (89 shorter events, 49.1 us)
Async XLA Ops:
  0.0 23.5 %collective-permute-start.1 = (bf16[128,3584]{1,0:T(8,128)(2,1)}, bf16[128,3584]{1,0:T(8,128)(2,1)S(1)}, u32[]{:S(2)}, u32[]{:S(2)}) collective-permute-start(bf16[128,3584]{1,0:T(8,128)(2,1)} %refs_0_.7), channel_id=1, source_target_pairs={{0,2},{1,3},{2,0},{3,1},{4,6},{5,7},{6,4},{7,5},{8,10},{9,11},{10,... | collective-permute-start | bytes 2752520 | tf_op jit(solution)/shard_map/ppermute | solution.py:17
  3.0 20.6 %collective-permute-start = (bf16[128,3584]{1,0:T(8,128)(2,1)}, bf16[128,3584]{1,0:T(8,128)(2,1)S(1)}, u32[]{:S(2)}, u32[]{:S(2)}) collective-permute-start(bf16[128,3584]{1,0:T(8,128)(2,1)} %refs_0_.7), channel_id=1, source_target_pairs={{0,1},{1,0},{2,3},{3,2},{4,5},{5,4},{6,7},{7,6},{8,9},{9,8},{10,11... | collective-permute-start | bytes 2752520 | tf_op jit(solution)/shard_map/ppermute | solution.py:17
  23.5 26.0 %collective-permute-start.2 = (bf16[128,3584]{1,0:T(8,128)(2,1)S(1)}, bf16[128,3584]{1,0:T(8,128)(2,1)S(1)}, u32[]{:S(2)}, u32[]{:S(2)}) collective-permute-start(bf16[128,3584]{1,0:T(8,128)(2,1)S(1)} %collective-permute-done.1.refs_2_.refs_0_), channel_id=1, source_target_pairs={{0,1},{1,0},{2,3},{3,2},{4,5},{5,4},{6,7},{7,6},{8,9},{9,8},{10,11... | collective-permute-start | bytes 2752520 | tf_op jit(solution)/shard_map/ppermute | solution.py:17
  33.4 93.6 %collective-permute-start.6 = (f32[64,7168]{1,0:T(8,128)S(1)}, f32[64,7168]{1,0:T(8,128)S(1)}, u32[]{:S(2)}, u32[]{:S(2)}) collective-permute-start(f32[64,7168]{1,0:T(8,128)S(1)} %copy-done), channel_id=1, source_target_pairs={{0,8},{4,12},{24,16},{28,20},{1,9},{5,13},{25,17},{29,21},{2,10},{... | collective-permute-start | bytes 5505032 | tf_op jit(solution)/shard_map/ppermute | solution.py:334
  43.6 54.0 %collective-permute-start.18 = (bf16[128,1792]{1,0:T(8,128)(2,1)S(1)}, bf16[128,1792]{1,0:T(8,128)(2,1)S(1)}, u32[]{:S(2)}, u32[]{:S(2)}) collective-permute-start(bf16[128,1792]{1,0:T(8,128)(2,1)S(1)} %get-tuple-element.56), channel_id=1, source_target_pairs={{0,4},{4,0},{8,12},{12,8},{16,20},{20,16},{24,28},{28,24},{1,5},{5... | collective-permute-start | bytes 1376264 | tf_op jit(solution)/shard_map/ppermute | solution.py:17
  45.2 41.9 %collective-permute-start.28 = (bf16[128,1792]{1,0:T(8,128)(2,1)S(1)}, bf16[128,1792]{1,0:T(8,128)(2,1)S(1)}, u32[]{:S(2)}, u32[]{:S(2)}) collective-permute-start(bf16[128,1792]{1,0:T(8,128)(2,1)S(1)} %shard_map.55), channel_id=1, source_target_pairs={{0,8},{4,12},{24,16},{28,20},{1,9},{5,13},{25,17},{29,21},{2,10},{... | collective-permute-start | bytes 1376264 | tf_op jit(solution)/shard_map/ppermute | solution.py:334
  67.7 55.2 %collective-permute-start.3 = (bf16[256,1792]{1,0:T(8,128)(2,1)S(1)}, bf16[256,1792]{1,0:T(8,128)(2,1)S(1)}, u32[]{:S(2)}, u32[]{:S(2)}) collective-permute-start(bf16[256,1792]{1,0:T(8,128)(2,1)S(1)} %get-tuple-element.46), channel_id=1, source_target_pairs={{0,4},{4,0},{8,12},{12,8},{16,20},{20,16},{24,28},{28,24},{1,5},{5... | collective-permute-start | bytes 2752520 | tf_op jit(solution)/shard_map/ppermute | solution.py:17
  68.9 27.3 %collective-permute-start.30 = (bf16[128,1792]{1,0:T(8,128)(2,1)S(1)}, bf16[128,1792]{1,0:T(8,128)(2,1)S(1)}, u32[]{:S(2)}, u32[]{:S(2)}) collective-permute-start(bf16[128,1792]{1,0:T(8,128)(2,1)S(1)} %shard_map.57), channel_id=1, source_target_pairs={{0,8},{4,12},{24,16},{28,20},{1,9},{5,13},{25,17},{29,21},{2,10},{... | collective-permute-start | bytes 1376264 | tf_op jit(solution)/shard_map/ppermute | solution.py:334
  87.1 37.8 %collective-permute-start.11 = (bf16[256,1792]{1,0:T(8,128)(2,1)S(1)}, bf16[256,1792]{1,0:T(8,128)(2,1)S(1)}, u32[]{:S(2)}, u32[]{:S(2)}) collective-permute-start(bf16[256,1792]{1,0:T(8,128)(2,1)S(1)} %get-tuple-element.51), channel_id=1, source_target_pairs={{0,4},{4,0},{8,12},{12,8},{16,20},{20,16},{24,28},{28,24},{1,5},{5... | collective-permute-start | bytes 2752520 | tf_op jit(solution)/shard_map/ppermute | solution.py:17
  96.2 21.9 %collective-permute-start.20 = (bf16[128,1792]{1,0:T(8,128)(2,1)S(1)}, bf16[128,1792]{1,0:T(8,128)(2,1)S(1)}, u32[]{:S(2)}, u32[]{:S(2)}) collective-permute-start(bf16[128,1792]{1,0:T(8,128)(2,1)S(1)} %get-tuple-element.58), channel_id=1, source_target_pairs={{0,4},{4,0},{8,12},{12,8},{16,20},{20,16},{24,28},{28,24},{1,5},{5... | collective-permute-start | bytes 1376264 | tf_op jit(solution)/shard_map/ppermute | solution.py:17
  97.6 30.7 %collective-permute-start.31 = (bf16[128,1792]{1,0:T(8,128)(2,1)S(1)}, bf16[128,1792]{1,0:T(8,128)(2,1)S(1)}, u32[]{:S(2)}, u32[]{:S(2)}) collective-permute-start(bf16[128,1792]{1,0:T(8,128)(2,1)S(1)} %get-tuple-element.66), channel_id=1, source_target_pairs={{8,16},{12,20},{16,8},{20,12},{9,17},{13,21},{17,9},{21,13},{10,18... | collective-permute-start | bytes 1376264 | tf_op jit(solution)/shard_map/ppermute | solution.py:334
  122.8 20.1 %collective-permute-start.21 = (bf16[128,1792]{1,0:T(8,128)(2,1)S(1)}, bf16[128,1792]{1,0:T(8,128)(2,1)S(1)}, u32[]{:S(2)}, u32[]{:S(2)}) collective-permute-start(bf16[128,1792]{1,0:T(8,128)(2,1)S(1)} %shard_map.50), channel_id=1, source_target_pairs={{0,8},{4,12},{24,16},{28,20},{1,9},{5,13},{25,17},{29,21},{2,10},{... | collective-permute-start | bytes 1376264 | tf_op jit(solution)/shard_map/ppermute | solution.py:334
  124.9 37.7 %collective-permute-start.4 = (bf16[256,1792]{1,0:T(8,128)(2,1)S(1)}, bf16[256,1792]{1,0:T(8,128)(2,1)S(1)}, u32[]{:S(2)}, u32[]{:S(2)}) collective-permute-start(bf16[256,1792]{1,0:T(8,128)(2,1)S(1)} %shard_map.38), channel_id=1, source_target_pairs={{0,8},{4,12},{24,16},{28,20},{1,9},{5,13},{25,17},{29,21},{2,10},{... | collective-permute-start | bytes 2752520 | tf_op jit(solution)/shard_map/ppermute | solution.py:334
  126.9 52.1 %collective-permute-start.12 = (bf16[256,1792]{1,0:T(8,128)(2,1)S(1)}, bf16[256,1792]{1,0:T(8,128)(2,1)S(1)}, u32[]{:S(2)}, u32[]{:S(2)}) collective-permute-start(bf16[256,1792]{1,0:T(8,128)(2,1)S(1)} %shard_map.43), channel_id=1, source_target_pairs={{0,8},{4,12},{24,16},{28,20},{1,9},{5,13},{25,17},{29,21},{2,10},{... | collective-permute-start | bytes 2752520 | tf_op jit(solution)/shard_map/ppermute | solution.py:334
  129.0 16.8 %collective-permute-start.32 = (bf16[128,1792]{1,0:T(8,128)(2,1)S(1)}, bf16[128,1792]{1,0:T(8,128)(2,1)S(1)}, u32[]{:S(2)}, u32[]{:S(2)}) collective-permute-start(bf16[128,1792]{1,0:T(8,128)(2,1)S(1)} %shard_map.59.near), channel_id=1, source_target_pairs={{8,16},{12,20},{16,8},{20,12},{9,17},{13,21},{17,9},{21,13},{10,18... | collective-permute-start | bytes 1376264 | tf_op jit(solution)/shard_map/ppermute | solution.py:334
  144.5 36.2 %collective-permute-start.33 = (bf16[128,1792]{1,0:T(8,128)(2,1)S(1)}, bf16[128,1792]{1,0:T(8,128)(2,1)S(1)}, u32[]{:S(2)}, u32[]{:S(2)}) collective-permute-start(bf16[128,1792]{1,0:T(8,128)(2,1)S(1)} %shard_map.59.near), channel_id=1, source_target_pairs={{8,0},{12,4},{16,24},{20,28},{9,1},{13,5},{17,25},{21,29},{10,2},{... | collective-permute-start | bytes 1376264 | tf_op jit(solution)/shard_map/ppermute | solution.py:334
  145.8 34.9 %collective-permute-start.34 = (bf16[128,1792]{1,0:T(8,128)(2,1)S(1)}, bf16[128,1792]{1,0:T(8,128)(2,1)S(1)}, u32[]{:S(2)}, u32[]{:S(2)}) collective-permute-start(bf16[128,1792]{1,0:T(8,128)(2,1)S(1)} %collective-permute-done.32.away), channel_id=1, source_target_pairs={{8,0},{12,4},{16,24},{20,28},{9,1},{13,5},{17,25},{21,29},{10,2},{... | collective-permute-start | bytes 1376264 | tf_op jit(solution)/shard_map/ppermute | solution.py:334
  147.8 35.4 %collective-permute-start.23 = (bf16[128,1792]{1,0:T(8,128)(2,1)S(1)}, bf16[128,1792]{1,0:T(8,128)(2,1)S(1)}, u32[]{:S(2)}, u32[]{:S(2)}) collective-permute-start(bf16[128,1792]{1,0:T(8,128)(2,1)S(1)} %shard_map.52.near), channel_id=1, source_target_pairs={{8,16},{12,20},{16,8},{20,12},{9,17},{13,21},{17,9},{21,13},{10,18... | collective-permute-start | bytes 1376264 | tf_op jit(solution)/shard_map/ppermute | solution.py:334
  163.4 21.2 %collective-permute-start.5 = (bf16[128,1792]{1,0:T(8,128)(2,1)S(1)}, bf16[128,1792]{1,0:T(8,128)(2,1)S(1)}, u32[]{:S(2)}, u32[]{:S(2)}) collective-permute-start(bf16[128,1792]{1,0:T(8,128)(2,1)S(1)} %get-tuple-element.48), channel_id=1, source_target_pairs={{8,16},{12,20},{16,8},{20,12},{9,17},{13,21},{17,9},{21,13},{10,18... | collective-permute-start | bytes 1376264 | tf_op jit(solution)/shard_map/ppermute | solution.py:334
  181.4 30.1 %collective-permute-start.35 = (bf16[256,1792]{1,0:T(8,128)(2,1)S(1)}, bf16[256,1792]{1,0:T(8,128)(2,1)S(1)}, u32[]{:S(2)}, u32[]{:S(2)}) collective-permute-start(bf16[256,1792]{1,0:T(8,128)(2,1)S(1)} %shard_map.60.lo), channel_id=1, source_target_pairs={{0,4},{4,0},{8,12},{12,8},{16,20},{20,16},{24,28},{28,24},{1,5},{5... | collective-permute-start | bytes 2752520 | tf_op jit(solution)/shard_map/ppermute | solution.py:17
  181.9 17.9 %collective-permute-start.24 = (bf16[128,1792]{1,0:T(8,128)(2,1)S(1)}, bf16[128,1792]{1,0:T(8,128)(2,1)S(1)}, u32[]{:S(2)}, u32[]{:S(2)}) collective-permute-start(bf16[128,1792]{1,0:T(8,128)(2,1)S(1)} %shard_map.52.near), channel_id=1, source_target_pairs={{8,0},{12,4},{16,24},{20,28},{9,1},{13,5},{17,25},{21,29},{10,2},{... | collective-permute-start | bytes 1376264 | tf_op jit(solution)/shard_map/ppermute | solution.py:334
  183.2 22.1 %collective-permute-start.25 = (bf16[128,1792]{1,0:T(8,128)(2,1)S(1)}, bf16[128,1792]{1,0:T(8,128)(2,1)S(1)}, u32[]{:S(2)}, u32[]{:S(2)}) collective-permute-start(bf16[128,1792]{1,0:T(8,128)(2,1)S(1)} %collective-permute-done.23.away), channel_id=1, source_target_pairs={{8,0},{12,4},{16,24},{20,28},{9,1},{13,5},{17,25},{21,29},{10,2},{... | collective-permute-start | bytes 1376264 | tf_op jit(solution)/shard_map/ppermute | solution.py:334
  185.3 23.6 %collective-permute-start.7 = (bf16[128,1792]{1,0:T(8,128)(2,1)S(1)}, bf16[128,1792]{1,0:T(8,128)(2,1)S(1)}, u32[]{:S(2)}, u32[]{:S(2)}) collective-permute-start(bf16[128,1792]{1,0:T(8,128)(2,1)S(1)} %shard_map.40.near), channel_id=1, source_target_pairs={{8,16},{12,20},{16,8},{20,12},{9,17},{13,21},{17,9},{21,13},{10,18... | collective-permute-start | bytes 1376264 | tf_op jit(solution)/shard_map/ppermute | solution.py:334
  186.7 23.5 %collective-permute-start.14 = (bf16[128,1792]{1,0:T(8,128)(2,1)S(1)}, bf16[128,1792]{1,0:T(8,128)(2,1)S(1)}, u32[]{:S(2)}, u32[]{:S(2)}) collective-permute-start(bf16[128,1792]{1,0:T(8,128)(2,1)S(1)} %shard_map.45.near), channel_id=1, source_target_pairs={{8,16},{12,20},{16,8},{20,12},{9,17},{13,21},{17,9},{21,13},{10,18... | collective-permute-start | bytes 1376264 | tf_op jit(solution)/shard_map/ppermute | solution.py:334
  206.0 42.1 %collective-permute-start.26 = (bf16[256,1792]{1,0:T(8,128)(2,1)S(1)}, bf16[256,1792]{1,0:T(8,128)(2,1)S(1)}, u32[]{:S(2)}, u32[]{:S(2)}) collective-permute-start(bf16[256,1792]{1,0:T(8,128)(2,1)S(1)} %shard_map.53.lo), channel_id=1, source_target_pairs={{0,4},{4,0},{8,12},{12,8},{16,20},{20,16},{24,28},{28,24},{1,5},{5... | collective-permute-start | bytes 2752520 | tf_op jit(solution)/shard_map/ppermute | solution.py:17
  208.9 34.3 %collective-permute-start.15 = (bf16[128,1792]{1,0:T(8,128)(2,1)S(1)}, bf16[128,1792]{1,0:T(8,128)(2,1)S(1)}, u32[]{:S(2)}, u32[]{:S(2)}) collective-permute-start(bf16[128,1792]{1,0:T(8,128)(2,1)S(1)} %shard_map.45.near), channel_id=1, source_target_pairs={{8,0},{12,4},{16,24},{20,28},{9,1},{13,5},{17,25},{21,29},{10,2},{... | collective-permute-start | bytes 1376264 | tf_op jit(solution)/shard_map/ppermute | solution.py:334
  210.2 31.8 %collective-permute-start.9 = (bf16[128,1792]{1,0:T(8,128)(2,1)S(1)}, bf16[128,1792]{1,0:T(8,128)(2,1)S(1)}, u32[]{:S(2)}, u32[]{:S(2)}) collective-permute-start(bf16[128,1792]{1,0:T(8,128)(2,1)S(1)} %collective-permute-done.7.away), channel_id=1, source_target_pairs={{8,0},{12,4},{16,24},{20,28},{9,1},{13,5},{17,25},{21,29},{10,2},{... | collective-permute-start | bytes 1376264 | tf_op jit(solution)/shard_map/ppermute | solution.py:334
  211.5 35.4 %collective-permute-start.16 = (bf16[128,1792]{1,0:T(8,128)(2,1)S(1)}, bf16[128,1792]{1,0:T(8,128)(2,1)S(1)}, u32[]{:S(2)}, u32[]{:S(2)}) collective-permute-start(bf16[128,1792]{1,0:T(8,128)(2,1)S(1)} %collective-permute-done.14.away), channel_id=1, source_target_pairs={{8,0},{12,4},{16,24},{20,28},{9,1},{13,5},{17,25},{21,29},{10,2},{... | collective-permute-start | bytes 1376264 | tf_op jit(solution)/shard_map/ppermute | solution.py:334
  242.6 28.1 %collective-permute-start.37 = (bf16[128,1792]{1,0:T(8,128)(2,1)S(1)}, bf16[128,1792]{1,0:T(8,128)(2,1)S(1)}, u32[]{:S(2)}, u32[]{:S(2)}) collective-permute-start(bf16[128,1792]{1,0:T(8,128)(2,1)S(1)} %get-tuple-element.77.lo), channel_id=1, source_target_pairs={{0,4},{4,0},{8,12},{12,8},{16,20},{20,16},{24,28},{28,24},{1,5},{5... | collective-permute-start | bytes 1376264 | tf_op jit(solution)/shard_map/ppermute | solution.py:17
  258.2 19.5 %collective-permute-start.17 = (bf16[128,1792]{1,0:T(8,128)(2,1)S(1)}, bf16[128,1792]{1,0:T(8,128)(2,1)S(1)}, u32[]{:S(2)}, u32[]{:S(2)}) collective-permute-start(bf16[128,1792]{1,0:T(8,128)(2,1)S(1)} %get-tuple-element.54.lo), channel_id=1, source_target_pairs={{0,4},{4,0},{8,12},{12,8},{16,20},{20,16},{24,28},{28,24},{1,5},{5... | collective-permute-start | bytes 1376264 | tf_op jit(solution)/shard_map/ppermute | solution.py:17
  277.6 19.9 %collective-permute-start.39 = (bf16[128,3584]{1,0:T(8,128)(2,1)S(1)}, bf16[128,3584]{1,0:T(8,128)(2,1)S(1)}, u32[]{:S(2)}, u32[]{:S(2)}) collective-permute-start(bf16[128,3584]{1,0:T(8,128)(2,1)S(1)} %get-tuple-element.84), channel_id=1, source_target_pairs={{0,1},{1,0},{2,3},{3,2},{4,5},{5,4},{6,7},{7,6},{8,9},{9,8},{10,11... | collective-permute-start | bytes 2752520 | tf_op jit(solution)/shard_map/ppermute | solution.py:17
  298.5 22.8 %collective-permute-start.40 = (bf16[128,3584]{1,0:T(8,128)(2,1)S(1)}, bf16[128,3584]{1,0:T(8,128)(2,1)S(1)}, u32[]{:S(2)}, u32[]{:S(2)}) collective-permute-start(bf16[128,3584]{1,0:T(8,128)(2,1)S(1)} %shard_map.67), channel_id=1, source_target_pairs={{0,2},{1,3},{2,0},{3,1},{4,6},{5,7},{6,4},{7,5},{8,10},{9,11},{10,... | collective-permute-start | bytes 2752520 | tf_op jit(solution)/shard_map/ppermute | solution.py:17
  (12 other events, 120.4 us)
